TPU v7x, 32 devices: a whole 2x2x4 slice. The times are simulated.
32 devices in a mesh: grp: 8 (over z, core), own: 4 (over y, x).
Axes of the slice: x: 2, y: 2, z: 4, core: 2. Of those that a mesh axis runs over, the one named last changes fastest.
Arguments:
- tokens: bfloat16 [8192, 1024], P(('grp', 'own')), may hold values from -6 to 6
- cotangent: bfloat16 [8192, 1024], P(('grp', 'own')), may hold values from -6 to 6
- doc_lengths: int32 [4, 4], replicated, may hold values from 256 to 1280, as said below
- w_in: float32 [1024, 3072], P('own', 'grp'), may hold values from -0.1875 to 0.1875
- w_out: float32 [1024, 1024], P('own', 'grp'), may hold values from -0.1875 to 0.1875
- w_gate: float32 [1024, 4608], P('own', 'grp'), may hold values from -0.1875 to 0.1875
- w_up: float32 [1024, 4608], P('own', 'grp'), may hold values from -0.1875 to 0.1875
- w_down: float32 [4608, 1024], P('own', 'grp'), may hold values from -0.09375 to 0.09375
- conv_w: float32 [3, 1024], P(None, 'own'), may hold values from -3.5 to 3.5
- gain: float32 [1024], P('own'), may hold values from 0.5 to 1.5
- gain_two: float32 [1024], P('own'), may hold values from 0.5 to 1.5
- moment_in: float32 [1024, 3072], P('own', 'grp'), as said below
- moment_out: float32 [1024, 1024], P('own', 'grp'), as said below
- moment_gate: float32 [1024, 4608], P('own', 'grp'), as said below
- moment_up: float32 [1024, 4608], P('own', 'grp'), as said below
- moment_down: float32 [4608, 1024], P('own', 'grp'), as said below
- moment_conv: float32 [3, 1024], P(None, 'own'), as said below
- moment_gain: float32 [1024], P('own'), as said below
- moment_gain_two: float32 [1024], P('own'), as said below
- square_in: float32 [1024, 3072], P('own', 'grp'), as said below
- square_out: float32 [1024, 1024], P('own', 'grp'), as said below
- square_gate: float32 [1024, 4608], P('own', 'grp'), as said below
- square_up: float32 [1024, 4608], P('own', 'grp'), as said below
- square_down: float32 [4608, 1024], P('own', 'grp'), as said below
- square_conv: float32 [3, 1024], P(None, 'own'), as said below
- square_gain: float32 [1024], P('own'), as said below
- square_gain_two: float32 [1024], P('own'), as said below
Outputs:
- block_out: bfloat16 [8192, 1024], P(('grp', 'own'))
- grad_tokens: bfloat16 [8192, 1024], P(('grp', 'own'))
- grad_w_in: float32 [1024, 3072], P('own')
- grad_w_out: float32 [1024, 1024], P('own')
- grad_w_gate: float32 [1024, 4608], P('own')
- grad_w_up: float32 [1024, 4608], P('own')
- grad_w_down: float32 [4608, 1024], P('own')
- grad_conv_w: float32 [3, 1024], P(None, 'own')
- grad_gain: float32 [1024], P('own')
- grad_gain_two: float32 [1024], P('own')
- new_w_in: float32 [1024, 3072], P('own', 'grp')
- new_w_out: float32 [1024, 1024], P('own', 'grp')
- new_w_gate: float32 [1024, 4608], P('own', 'grp')
- new_w_up: float32 [1024, 4608], P('own', 'grp')
- new_w_down: float32 [4608, 1024], P('own', 'grp')
- new_conv_w: float32 [3, 1024], P(None, 'own')
- new_gain: float32 [1024], P('own')
- new_gain_two: float32 [1024], P('own')
- new_moment_in: float32 [1024, 3072], P('own', 'grp')
- new_moment_out: float32 [1024, 1024], P('own', 'grp')
- new_moment_gate: float32 [1024, 4608], P('own', 'grp')
- new_moment_up: float32 [1024, 4608], P('own', 'grp')
- new_moment_down: float32 [4608, 1024], P('own', 'grp')
- new_moment_conv: float32 [3, 1024], P(None, 'own')
- new_moment_gain: float32 [1024], P('own')
- new_moment_gain_two: float32 [1024], P('own')
- new_square_in: float32 [1024, 3072], P('own', 'grp')
- new_square_out: float32 [1024, 1024], P('own', 'grp')
- new_square_gate: float32 [1024, 4608], P('own', 'grp')
- new_square_up: float32 [1024, 4608], P('own', 'grp')
- new_square_down: float32 [4608, 1024], P('own', 'grp')
- new_square_conv: float32 [3, 1024], P(None, 'own')
- new_square_gain: float32 [1024], P('own')
- new_square_gain_two: float32 [1024], P('own')
Inputs may be any that keep to these rules, and one draw needn't show every extreme that they name: `doc_lengths`: the 4 lengths of each sequence sum to 2048. `moment_in`: first moments: real values of either sign. `moment_out`: first moments: real values of either sign. `moment_gate`: first moments: real values of either sign. `moment_up`: first moments: real values of either sign. `moment_down`: first moments: real values of either sign. `moment_conv`: first moments: real values of either sign. `moment_gain`: first moments: real values of either sign. `moment_gain_two`: first moments: real values of either sign. `square_in`: second moments are positive. `square_out`: second moments are positive. `square_gate`: second moments are positive. `square_up`: second moments are positive. `square_down`: second moments are positive. `square_conv`: second moments are positive. `square_gain`: second moments are positive. `square_gain_two`: second moments are positive.
All inputs are finite; a program needn't handle non-finite values.
Results may differ from a plain program's by a relative error of at most 0.025.
Values may be sent and summed in bfloat16 or wider, within the bound.
No kernel may reach another device: no remote copies, remote signals or barrier semaphores. Data moves between devices by JAX's collectives and lax.ppermute only.
A program may use at most 320 MiB of HBM per device.

v0:
```python
import jax
import jax.numpy as jnp
from jax import lax
from jax.sharding import PartitionSpec as P

SEQ_LEN = 2048


eps_norm = 1e-05
eps_adam = 1e-08
beta_one = 0.9
beta_two = 0.95
train_step = 5
rate_matrix = 0.004
rate_vector = 0.1
decay_matrix = 0.1


def passed_along(block, axis, distance):
    devices = range(lax.axis_size(axis))
    route = [(i - distance, i) for i in devices if i - distance in devices]
    return lax.ppermute(block, axis, route)


def stream_starts(doc_lengths, seq_len):
    starts = jnp.cumsum(doc_lengths, axis=1) - doc_lengths
    base = (jnp.arange(doc_lengths.shape[0], dtype=jnp.int32) * seq_len)[:, None]
    first = (jnp.arange(doc_lengths.shape[1], dtype=jnp.int32) == 0)[None, :]
    return jnp.where(first, 0, base + starts).reshape(-1)


def since_start(positions, stream):
    below = jnp.where(stream[None, :] <= positions[:, None], stream[None, :], 0)
    return positions - jnp.max(below, axis=1)


def apply_adam(param, first, second, grad, rate, decay):
    first_new = beta_one * first + (1.0 - beta_one) * grad
    second_new = beta_two * second + (1.0 - beta_two) * grad * grad
    first_hat = first_new / (1.0 - beta_one**train_step)
    second_hat = second_new / (1.0 - beta_two**train_step)
    param_new = param - rate * (first_hat / (jnp.sqrt(second_hat) + eps_adam) + decay * param)
    return (param_new, first_new, second_new)


def local(
    tokens,
    cotangent,
    doc_lengths,
    w_in,
    w_out,
    w_gate,
    w_up,
    w_down,
    conv_w,
    gain,
    gain_two,
    moment_in,
    moment_out,
    moment_gate,
    moment_up,
    moment_down,
    moment_conv,
    moment_gain,
    moment_gain_two,
    square_in,
    square_out,
    square_gate,
    square_up,
    square_down,
    square_conv,
    square_gain,
    square_gain_two,
):
    across = (
        lax.all_gather(w_in.astype(jnp.bfloat16), "grp", axis=1, tiled=True),
        lax.all_gather(w_out.astype(jnp.bfloat16), "grp", axis=1, tiled=True),
        lax.all_gather(w_gate.astype(jnp.bfloat16), "grp", axis=1, tiled=True),
        lax.all_gather(w_up.astype(jnp.bfloat16), "grp", axis=1, tiled=True),
        lax.all_gather(w_down.astype(jnp.bfloat16), "grp", axis=1, tiled=True),
    )
    in_half, out_half, gate_half, up_half, down_half, conv_half, gain_half, gain_two_half = (
        lax.all_gather(across[0], "own", axis=0, tiled=True),
        lax.all_gather(across[1], "own", axis=0, tiled=True),
        lax.all_gather(across[2], "own", axis=0, tiled=True),
        lax.all_gather(across[3], "own", axis=0, tiled=True),
        lax.all_gather(across[4], "own", axis=0, tiled=True),
        lax.all_gather(conv_w.astype(jnp.bfloat16), "own", axis=1, tiled=True),
        lax.all_gather(gain.astype(jnp.bfloat16), "own", axis=0, tiled=True),
        lax.all_gather(gain_two.astype(jnp.bfloat16), "own", axis=0, tiled=True),
    )
    conv_float = conv_half.astype(jnp.float32)
    gain_float = gain_half.astype(jnp.float32)
    gain_two_float = gain_two_half.astype(jnp.float32)
    rows, width = tokens.shape
    hidden_width = gate_half.shape[1]
    taps = conv_half.shape[0]
    device = lax.axis_index(("grp", "own"))
    first_row = device * rows
    stream = stream_starts(doc_lengths, SEQ_LEN)
    position = first_row + jnp.arange(rows + taps - 1, dtype=jnp.int32)
    since = since_start(position, stream)
    x_float = tokens.astype(jnp.float32)
    cot_float = cotangent.astype(jnp.float32)
    inv_rms = lax.rsqrt(jnp.mean(x_float * x_float, axis=1, keepdims=True) + eps_norm)
    normed = (x_float * inv_rms * gain_float).astype(jnp.bfloat16)
    project = jnp.dot(normed, in_half, preferred_element_type=jnp.float32)
    b_gate = project[:, :width]
    c_gate = project[:, width : 2 * width]
    x_value = project[:, 2 * width :]
    gated = b_gate * x_value
    before = passed_along(gated[rows - taps + 1 :], ("grp", "own"), 1)
    extended = jnp.concatenate([before, gated], 0)
    convolved = jnp.zeros((rows, width), jnp.float32)
    for tap_index in range(taps):
        keep = (since[:rows] >= tap_index)[:, None]
        moved = extended[taps - 1 - tap_index : taps - 1 - tap_index + rows]
        convolved = convolved + jnp.where(keep, conv_float[tap_index] * moved, 0.0)
    mixed = (c_gate * convolved).astype(jnp.bfloat16)
    middle = x_float + jnp.dot(mixed, out_half, preferred_element_type=jnp.float32)
    inv_two = lax.rsqrt(jnp.mean(middle * middle, axis=1, keepdims=True) + eps_norm)
    normed_two = (middle * inv_two * gain_two_float).astype(jnp.bfloat16)
    gate = jnp.dot(normed_two, gate_half, preferred_element_type=jnp.float32)
    up = jnp.dot(normed_two, up_half, preferred_element_type=jnp.float32)
    sig = jax.nn.sigmoid(gate)
    activated = gate * sig
    hidden = (activated * up).astype(jnp.bfloat16)
    block_out = (middle + jnp.dot(hidden, down_half, preferred_element_type=jnp.float32)).astype(
        jnp.bfloat16
    )
    grad_hidden = jnp.dot(cotangent, down_half.T, preferred_element_type=jnp.float32)
    grad_gate = (grad_hidden * up * sig * (1.0 + gate * (1.0 - sig))).astype(jnp.bfloat16)
    grad_up = (grad_hidden * activated).astype(jnp.bfloat16)
    grad_normed_two = jnp.dot(grad_gate, gate_half.T, preferred_element_type=jnp.float32) + jnp.dot(
        grad_up, up_half.T, preferred_element_type=jnp.float32
    )
    gain_two_rows = jnp.sum(grad_normed_two * middle * inv_two, axis=0)
    weighted_two = gain_two_float * grad_normed_two
    grad_middle = (
        cot_float
        + inv_two * weighted_two
        - middle
        * inv_two
        * inv_two
        * inv_two
        * jnp.mean(weighted_two * middle, axis=1, keepdims=True)
    )
    grad_middle_half = grad_middle.astype(jnp.bfloat16)
    grad_mixed = jnp.dot(grad_middle_half, out_half.T, preferred_element_type=jnp.float32)
    grad_c = grad_mixed * convolved
    grad_conv = grad_mixed * c_gate
    after = passed_along(grad_conv[: taps - 1], ("grp", "own"), -1)
    grad_extended = jnp.concatenate([grad_conv, after], 0)
    grad_gated = jnp.zeros((rows, width), jnp.float32)
    tap_sums = []
    for tap_index in range(taps):
        keep_ahead = (since[tap_index : tap_index + rows] >= tap_index)[:, None]
        grad_gated = grad_gated + conv_float[tap_index] * jnp.where(
            keep_ahead, grad_extended[tap_index : tap_index + rows], 0.0
        )
        keep = (since[:rows] >= tap_index)[:, None]
        moved = extended[taps - 1 - tap_index : taps - 1 - tap_index + rows]
        tap_sums.append(jnp.sum(jnp.where(keep, grad_conv * moved, 0.0), axis=0))
    grad_b = grad_gated * x_value
    grad_x = grad_gated * b_gate
    grad_project = jnp.concatenate([grad_b, grad_c, grad_x], 1).astype(jnp.bfloat16)
    grad_normed = jnp.dot(grad_project, in_half.T, preferred_element_type=jnp.float32)
    gain_rows = jnp.sum(grad_normed * x_float * inv_rms, axis=0)
    weighted = gain_float * grad_normed
    grad_tokens = (
        grad_middle
        + inv_rms * weighted
        - x_float
        * inv_rms
        * inv_rms
        * inv_rms
        * jnp.mean(weighted * x_float, axis=1, keepdims=True)
    ).astype(jnp.bfloat16)
    small_terms = jnp.stack(tap_sums + [gain_rows, gain_two_rows], axis=1)
    wide_terms = jnp.concatenate(
        [
            jnp.dot(normed.T, grad_project, preferred_element_type=jnp.float32),
            jnp.dot(mixed.T, grad_middle_half, preferred_element_type=jnp.float32),
            jnp.dot(normed_two.T, grad_gate, preferred_element_type=jnp.float32),
            jnp.dot(normed_two.T, grad_up, preferred_element_type=jnp.float32),
        ],
        1,
    )
    down_terms = jnp.dot(hidden.T, cotangent, preferred_element_type=jnp.float32)
    shares = (
        lax.psum_scatter(
            wide_terms.astype(jnp.bfloat16), "own", scatter_dimension=0, tiled=True
        ).astype(jnp.float32),
        lax.psum_scatter(
            down_terms.astype(jnp.bfloat16), "own", scatter_dimension=0, tiled=True
        ).astype(jnp.float32),
        lax.psum_scatter(
            small_terms.astype(jnp.bfloat16), "own", scatter_dimension=0, tiled=True
        ).astype(jnp.float32),
    )
    wide_share, down_share, small_share = (
        lax.psum(shares[0].astype(jnp.bfloat16), "grp").astype(jnp.float32),
        lax.psum(shares[1].astype(jnp.bfloat16), "grp").astype(jnp.float32),
        lax.psum(shares[2].astype(jnp.bfloat16), "grp").astype(jnp.float32),
    )
    grad_w_in = wide_share[:, : 3 * width]
    grad_w_out = wide_share[:, 3 * width : 4 * width]
    grad_w_gate = wide_share[:, 4 * width : 4 * width + hidden_width]
    grad_w_up = wide_share[:, 4 * width + hidden_width :]
    grad_conv_w = small_share[:, :taps].T
    grad_gain = small_share[:, taps]
    grad_gain_two = small_share[:, taps + 1]
    column = lax.axis_index("grp")

    def own_columns(grad, param):
        count = param.shape[1]
        return lax.dynamic_slice_in_dim(grad, column * count, count, 1)

    new_w_in, new_moment_in, new_square_in = apply_adam(
        w_in, moment_in, square_in, own_columns(grad_w_in, w_in), rate_matrix, decay_matrix
    )
    new_w_out, new_moment_out, new_square_out = apply_adam(
        w_out, moment_out, square_out, own_columns(grad_w_out, w_out), rate_matrix, decay_matrix
    )
    new_w_gate, new_moment_gate, new_square_gate = apply_adam(
        w_gate,
        moment_gate,
        square_gate,
        own_columns(grad_w_gate, w_gate),
        rate_matrix,
        decay_matrix,
    )
    new_w_up, new_moment_up, new_square_up = apply_adam(
        w_up, moment_up, square_up, own_columns(grad_w_up, w_up), rate_matrix, decay_matrix
    )
    new_w_down, new_moment_down, new_square_down = apply_adam(
        w_down, moment_down, square_down, own_columns(down_share, w_down), rate_matrix, decay_matrix
    )
    new_conv_w, new_moment_conv, new_square_conv = apply_adam(
        conv_w, moment_conv, square_conv, grad_conv_w, rate_vector, 0.0
    )
    new_gain, new_moment_gain, new_square_gain = apply_adam(
        gain, moment_gain, square_gain, grad_gain, rate_vector, 0.0
    )
    new_gain_two, new_moment_gain_two, new_square_gain_two = apply_adam(
        gain_two, moment_gain_two, square_gain_two, grad_gain_two, rate_vector, 0.0
    )
    return (
        block_out,
        grad_tokens,
        grad_w_in,
        grad_w_out,
        grad_w_gate,
        grad_w_up,
        down_share,
        grad_conv_w,
        grad_gain,
        grad_gain_two,
        new_w_in,
        new_w_out,
        new_w_gate,
        new_w_up,
        new_w_down,
        new_conv_w,
        new_gain,
        new_gain_two,
        new_moment_in,
        new_moment_out,
        new_moment_gate,
        new_moment_up,
        new_moment_down,
        new_moment_conv,
        new_moment_gain,
        new_moment_gain_two,
        new_square_in,
        new_square_out,
        new_square_gate,
        new_square_up,
        new_square_down,
        new_square_conv,
        new_square_gain,
        new_square_gain_two,
    )


def solution(mesh):
    placed = (
        P(("grp", "own"), None),
        P(("grp", "own"), None),
        P(),
        P("own", "grp"),
        P("own", "grp"),
        P("own", "grp"),
        P("own", "grp"),
        P("own", "grp"),
        P(None, "own"),
        P("own"),
        P("own"),
        P("own", "grp"),
        P("own", "grp"),
        P("own", "grp"),
        P("own", "grp"),
        P("own", "grp"),
        P(None, "own"),
        P("own"),
        P("own"),
        P("own", "grp"),
        P("own", "grp"),
        P("own", "grp"),
        P("own", "grp"),
        P("own", "grp"),
        P(None, "own"),
        P("own"),
        P("own"),
    )
    return jax.shard_map(
        local,
        mesh=mesh,
        in_specs=placed,
        out_specs=(
            P(("grp", "own"), None),
            P(("grp", "own"), None),
            P("own", None),
            P("own", None),
            P("own", None),
            P("own", None),
            P("own", None),
            P(None, "own"),
            P("own"),
            P("own"),
            P("own", "grp"),
            P("own", "grp"),
            P("own", "grp"),
            P("own", "grp"),
            P("own", "grp"),
            P(None, "own"),
            P("own"),
            P("own"),
            P("own", "grp"),
            P("own", "grp"),
            P("own", "grp"),
            P("own", "grp"),
            P("own", "grp"),
            P(None, "own"),
            P("own"),
            P("own"),
            P("own", "grp"),
            P("own", "grp"),
            P("own", "grp"),
            P("own", "grp"),
            P("own", "grp"),
            P(None, "own"),
            P("own"),
            P("own"),
        ),
        check_vma=False,
    )
```

profile of v0, /device:TPU:0, one launch (start us, length us, event | category | flops | bytes accessed | tf_op | source)
XLA Modules:
  0.0 1173.6 jit_solution(15216509789549518167)
XLA Ops:
  14.7 23.3 %all-gather.12.cloned.1.call-done = bf16[256,3072]{1,0:T(8,128)(2,1)} async-done(((bf16[256,384]{1,0:T(8,128)(2,1)}), bf16[256,3072]{1,0:T(8,128)(2,1)}) %all-gather.12.cloned.1.call-update) | async-done | bytes 1572880 | tf_op jit(solution)/shard_map/all_gather | solution.py:76
  38.1 14.9 %all_gather.43 = bf16[256,1024]{1,0:T(8,128)(2,1)} all-gather(bf16[256,128]{1,0:T(8,128)(2,1)S(1)} %convert_element_type.95), channel_id=1, replica_groups=mesh['grp'=8,'own'=4] {'grp'}, dimensions={1}, use_global_device_ids=true | all-gather | bytes 589824 | tf_op jit(solution)/shard_map/all_gather | solution.py:77
  53.1 18.9 %all-gather.18.cloned.1.call-done = bf16[256,4608]{0,1:T(8,128)(2,1)} async-done(((bf16[256,576]{0,1:T(8,128)(2,1)}), bf16[256,4608]{0,1:T(8,128)(2,1)}) %all-gather.18.cloned.1.call-update) | async-done | bytes 2359312 | tf_op jit(solution)/shard_map/all_gather | solution.py:78
  72.1 32.5 %all-gather.22.cloned.1.call-done = bf16[256,4608]{0,1:T(8,128)(2,1)} async-done(((bf16[256,576]{0,1:T(8,128)(2,1)}), bf16[256,4608]{0,1:T(8,128)(2,1)}) %all-gather.22.cloned.1.call-update) | async-done | bytes 2359312 | tf_op jit(solution)/shard_map/all_gather | solution.py:79
  104.7 33.9 %all-gather.26.cloned.1.call-done = bf16[1152,1024]{1,0:T(8,128)(2,1)} async-done(((bf16[1152,128]{1,0:T(8,128)(2,1)}), bf16[1152,1024]{1,0:T(8,128)(2,1)}) %all-gather.26.cloned.1.call-update) | async-done | bytes 2359312 | tf_op jit(solution)/shard_map/all_gather | solution.py:80
  138.7 8.0 all-gather
  147.2 8.3 all_gather.42
  155.9 53.3 %all-gather.14.cloned.1.call-done = bf16[1024,3072]{1,0:T(8,128)(2,1)} async-done(((bf16[256,3072]{1,0:T(8,128)(2,1)}), bf16[1024,3072]{1,0:T(8,128)(2,1)}) %all-gather.14.cloned.1.call-update) | async-done | bytes 6291472 | tf_op jit(solution)/shard_map/all_gather | solution.py:83
  209.2 4.7 fusion.30
  217.5 8.4 all-gather.1
  227.4 18.7 %all-gather.16.cloned.1.call-done = bf16[1024,1024]{1,0:T(8,128)(2,1)} async-done(((bf16[256,1024]{1,0:T(8,128)(2,1)}), bf16[1024,1024]{1,0:T(8,128)(2,1)}) %all-gather.16.cloned.1.call-update) | async-done | bytes 2097168 | tf_op jit(solution)/shard_map/all_gather | solution.py:84
  248.7 95.3 %all-gather.20.cloned.1.call-done = bf16[1024,4608]{0,1:T(8,128)(2,1)} async-done(((bf16[256,4608]{0,1:T(8,128)(2,1)}), bf16[1024,4608]{0,1:T(8,128)(2,1)}) %all-gather.20.cloned.1.call-update) | async-done | bytes 9437200 | tf_op jit(solution)/shard_map/all_gather | solution.py:85
  344.0 11.5 fusion.51
  355.5 86.4 %all-gather.24.cloned.1.call-done = bf16[1024,4608]{0,1:T(8,128)(2,1)} async-done(((bf16[256,4608]{0,1:T(8,128)(2,1)}), bf16[1024,4608]{0,1:T(8,128)(2,1)}) %all-gather.24.cloned.1.call-update) | async-done | bytes 9437200 | tf_op jit(solution)/shard_map/all_gather | solution.py:86
  441.9 11.5 fusion.52
  453.5 86.5 %all-gather.28.cloned.1.call-done = bf16[4608,1024]{1,0:T(8,128)(2,1)} async-done(((bf16[1152,1024]{1,0:T(8,128)(2,1)}), bf16[4608,1024]{1,0:T(8,128)(2,1)}) %all-gather.28.cloned.1.call-update) | async-done | bytes 9437200 | tf_op jit(solution)/shard_map/all_gather | solution.py:87
  540.0 13.8 %multiply_convert_fusion = (bf16[256,4608]{1,0:T(8,128)(2,1)}, bf16[256,4608]{1,0:T(8,128)(2,1)}, bf16[256,4608]{1,0:T(8,128)(2,1)S(1)}) fusion(f32[256,4608]{1,0:T(8,128)} %fusion.51, f32[256,4608]{1,0:T(8,128)} %fusion.52, bf16[256,1024]{1,0:T(8,128)(2,1)S(1)} %copy-done.16, bf16[4608,1024]{1,0:T(8,128)(2,1)} %all-gather.28.cloned.1.call-done), kind=kOutput, calls=%fused_computation.5 | convolution fusion | flops 2433613824 | bytes 26476544 | tf_op jit(solution)/shard_map/dot_general | solution.py:131
  555.2 5.0 convolution_convert_fusion
  560.6 6.0 fusion.53
  566.6 5.9 multiply_reduce_fusion
  577.2 5.1 convolution_convert_fusion.1
  582.3 5.2 convolution_convert_fusion.2
  595.6 31.4 %pad_maximum_fusion = bf16[1024,13312]{0,1:T(8,128)(2,1)} fusion(bf16[1024,4608]{0,1:T(8,128)(2,1)} %convolution_convert_fusion.1, bf16[1024,4608]{0,1:T(8,128)(2,1)} %convolution_convert_fusion.2, bf16[1024,1024]{0,1:T(8,128)(2,1)} %convolution_convert_fusion.4, bf16[1024,3072]{0,1:T(8,128)(2,1)} %convolution_convert_fusion.3), kind=kLoop, calls=%fused_computation | loop fusion | flops 109051904 | bytes 54525952 | tf_op jit(solution)/shard_map/concatenate | solution.py:180
  627.4 6.6 fusion.18
  634.8 20.7 %reduce-scatter.6.cloned.1.call-done = bf16[1152,1024]{1,0:T(8,128)(2,1)} async-done(((bf16[4608,1024]{1,0:T(8,128)(2,1)}), bf16[1152,1024]{1,0:T(8,128)(2,1)}) %reduce-scatter.6.cloned.1.call-update) | async-done | bytes 2359312 | tf_op jit(solution)/shard_map/reduce_scatter | solution.py:194
  655.5 241.9 %reduce-scatter.4.cloned.1.call-done = bf16[256,13312]{0,1:T(8,128)(2,1)} async-done(((bf16[1024,13312]{0,1:T(8,128)(2,1)}), bf16[256,13312]{0,1:T(8,128)(2,1)}) %reduce-scatter.4.cloned.1.call-update) | async-done | bytes 6815760 | tf_op jit(solution)/shard_map/reduce_scatter | solution.py:191
  906.2 7.9 fusion.1
  915.3 8.1 reduce-scatter.8.cloned.1.call-done
  923.4 16.4 %psum.23 = bf16[256,5]{0,1:T(8,128)(2,1)S(1)} all-reduce(bf16[256,5]{0,1:T(8,128)(2,1)} %reduce-scatter.8.cloned.1.call-done), channel_id=1, replica_groups=mesh['grp'=8,'own'=4] {'grp'}, use_global_device_ids=true, to_apply=%region_16.17 | all-reduce | flops 1280 | bytes 5120 | tf_op jit(solution)/shard_map/psum | solution.py:204
  941.1 175.2 %all-reduce.3.cloned.1.call-done = (bf16[256,13312]{0,1:T(8,128)(2,1)}, bf16[1152,1024]{1,0:T(8,128)(2,1)}) async-done(((bf16[256,13312]{0,1:T(8,128)(2,1)}, bf16[1152,1024]{1,0:T(8,128)(2,1)}), (bf16[256,13312]{0,1:T(8,128)(2,1)}, bf16[1152,1024]{1,0:T(8,128)(2,1)})) %all-reduce.3.cloned.1.call-update) | async-done | bytes 9175056 | tf_op jit(solution)/shard_map/psum | solution.py:202
  1129.9 6.0 copy.119
  1135.9 6.0 copy.120
  (191 shorter events, 81.2 us)
Async XLA Ops:
  7.2 30.8 %all-gather.12.cloned.1.call-start = ((), (), s32[]{:S(2)}) async-start(), calls=%async_computation.3 | async-start | bytes 1769472 | tf_op jit(solution)/shard_map/all_gather | solution.py:76
  9.0 63.0 %all-gather.18.cloned.1.call-start = ((), (), s32[]{:S(2)}) async-start(), calls=%async_computation.6 | async-start | bytes 2654208 | tf_op jit(solution)/shard_map/all_gather | solution.py:78
  10.9 93.7 %all-gather.22.cloned.1.call-start = ((), (), s32[]{:S(2)}) async-start(), calls=%async_computation.8 | async-start | bytes 2654208 | tf_op jit(solution)/shard_map/all_gather | solution.py:79
  12.8 125.8 %all-gather.26.cloned.1.call-start = ((), (), s32[]{:S(2)}) async-start(), calls=%async_computation.10 | async-start | bytes 2654208 | tf_op jit(solution)/shard_map/all_gather | solution.py:80
  14.7 194.5 %all-gather.14.cloned.1.call-start = ((), (), s32[]{:S(2)}) async-start(), calls=%async_computation.4 | async-start | bytes 7864320 | tf_op jit(solution)/shard_map/all_gather | solution.py:83
  38.0 100.7 %copy-start.36 = (f32[256]{0:T(256)S(1)}, f32[256]{0:T(256)}, u32[]{:S(2)}) copy-start(f32[256]{0:T(256)} %param.36) | copy-start | bytes 3076
  38.0 108.8 %copy-start.30 = (f32[3,256]{1,0:T(4,128)S(1)}, f32[3,256]{1,0:T(4,128)}, u32[]{:S(2)}) copy-start(f32[3,256]{1,0:T(4,128)} %param.35) | copy-start | bytes 9220
  38.0 108.8 %copy-start.31 = (s32[4,4]{1,0:T(4,128)S(1)}, s32[4,4]{1,0:T(4,128)}, u32[]{:S(2)}) copy-start(s32[4,4]{1,0:T(4,128)} %param.29) | copy-start | bytes 196
  38.0 117.6 %copy-start.6 = (bf16[256,1024]{1,0:T(8,128)(2,1)S(1)}, bf16[256,1024]{1,0:T(8,128)(2,1)}, u32[]{:S(2)}) copy-start(bf16[256,1024]{1,0:T(8,128)(2,1)} %param.27) | copy-start | bytes 1572868
  38.1 208.0 %all-gather.16.cloned.1.call-start = ((), (), s32[]{:S(2)}) async-start(), calls=%async_computation.5 | async-start | bytes 2621440 | tf_op jit(solution)/shard_map/all_gather | solution.py:84
  53.0 291.0 %all-gather.20.cloned.1.call-start = ((), (), s32[]{:S(2)}) async-start(), calls=%async_computation.7 | async-start | bytes 11796480 | tf_op jit(solution)/shard_map/all_gather | solution.py:85
  72.1 369.9 %all-gather.24.cloned.1.call-start = ((), (), s32[]{:S(2)}) async-start(), calls=%async_computation.9 | async-start | bytes 11796480 | tf_op jit(solution)/shard_map/all_gather | solution.py:86
  104.7 435.4 %all-gather.28.cloned.1.call-start = ((), (), s32[]{:S(2)}) async-start(), calls=%async_computation.11 | async-start | bytes 11796480 | tf_op jit(solution)/shard_map/all_gather | solution.py:87
  138.7 516.8 %reduce-scatter.6.cloned.1.call-start = ((), (), s32[]{:S(2)}) async-start(), calls=%async_computation.13 | async-start | bytes 11796480 | tf_op jit(solution)/shard_map/reduce_scatter | solution.py:194
  214.0 11.9 %collective-permute-start = (f32[2,1024]{1,0:T(2,128)S(1)}, f32[2,1024]{1,0:T(2,128)S(1)}, u32[]{:S(2)}, u32[]{:S(2)}) collective-permute-start(f32[2,1024]{1,0:T(2,128)S(1)} %slice.104), channel_id=1, source_target_pairs={{0,1},{1,2},{2,3},{3,4},{4,5},{5,6},{6,7},{7,8},{8,9},{9,10},{10,1... | collective-permute-start | bytes 24584 | tf_op jit(solution)/shard_map/ppermute | solution.py:22
  227.4 128.1 %copy-start.8 = (bf16[256,1024]{1,0:T(8,128)(2,1)}, bf16[256,1024]{1,0:T(8,128)(2,1)S(1)}, u32[]{:S(2)}) copy-start(bf16[256,1024]{1,0:T(8,128)(2,1)S(1)} %get-tuple-element.207) | copy-start | bytes 1572868
  248.7 193.3 %copy-start.4 = (bf16[256,1024]{1,0:T(8,128)(2,1)}, bf16[256,1024]{1,0:T(8,128)(2,1)S(1)}, u32[]{:S(2)}) copy-start(bf16[256,1024]{1,0:T(8,128)(2,1)S(1)} %multiply_convert_fusion.6) | copy-start | bytes 1572868
  441.9 98.1 %copy-start.16 = (bf16[256,1024]{1,0:T(8,128)(2,1)S(1)}, bf16[256,1024]{1,0:T(8,128)(2,1)}, u32[]{:S(2)}) copy-start(bf16[256,1024]{1,0:T(8,128)(2,1)} %param.28) | copy-start | bytes 1572868
  560.3 337.1 %reduce-scatter.4.cloned.1.call-start = ((), (), s32[]{:S(2)}) async-start(), calls=%async_computation.12 | async-start | bytes 34078720 | tf_op jit(solution)/shard_map/reduce_scatter | solution.py:191
  575.6 14.0 %collective-permute-start.1 = (f32[2,1024]{1,0:T(2,128)S(1)}, f32[2,1024]{1,0:T(2,128)S(1)}, u32[]{:S(2)}, u32[]{:S(2)}) collective-permute-start(f32[2,1024]{1,0:T(2,128)S(1)} %slice.108), channel_id=1, source_target_pairs={{1,0},{2,1},{3,2},{4,3},{5,4},{6,5},{7,6},{8,7},{9,8},{10,9},{11,1... | collective-permute-start | bytes 24584 | tf_op jit(solution)/shard_map/ppermute | solution.py:22
  627.0 296.4 %reduce-scatter.8.cloned.1.call-start = ((), (), s32[]{:S(2)}) async-start(), calls=%async_computation.14 | async-start | bytes 20480 | tf_op jit(solution)/shard_map/reduce_scatter | solution.py:197
  634.0 263.4 %copy-start.18 = (f32[256,384]{1,0:T(8,128)S(1)}, f32[256,384]{1,0:T(8,128)}, u32[]{:S(2)}) copy-start(f32[256,384]{1,0:T(8,128)} %param.30) | copy-start | bytes 1179652
  634.7 481.6 %all-reduce.3.cloned.1.call-start = ((), (), s32[]{:S(2)}) async-start(), calls=%async_computation.15 | async-start | bytes 18350080 | tf_op jit(solution)/shard_map/psum | solution.py:202
  906.2 33.7 %copy-start.38 = (f32[256]{0:T(256)S(1)}, f32[256]{0:T(256)}, u32[]{:S(2)}) copy-start(f32[256]{0:T(256)} %param.37) | copy-start | bytes 3076
  906.2 33.7 %copy-start.39 = (f32[256]{0:T(256)S(1)}, f32[256]{0:T(256)}, u32[]{:S(2)}) copy-start(f32[256]{0:T(256)} %param.45) | copy-start | bytes 3076
  906.2 33.7 %copy-start.40 = (f32[256]{0:T(256)S(1)}, f32[256]{0:T(256)}, u32[]{:S(2)}) copy-start(f32[256]{0:T(256)} %param.53) | copy-start | bytes 3076
  906.2 33.7 %copy-start.41 = (f32[256]{0:T(256)S(1)}, f32[256]{0:T(256)}, u32[]{:S(2)}) copy-start(f32[256]{0:T(256)} %param.52) | copy-start | bytes 3076
  906.2 33.7 %copy-start.42 = (f32[256]{0:T(256)S(1)}, f32[256]{0:T(256)}, u32[]{:S(2)}) copy-start(f32[256]{0:T(256)} %param.44) | copy-start | bytes 3076
  906.2 34.3 %copy-start.34 = (f32[3,256]{1,0:T(4,128)S(1)}, f32[3,256]{1,0:T(4,128)}, u32[]{:S(2)}) copy-start(f32[3,256]{1,0:T(4,128)} %param.43) | copy-start | bytes 9220
  906.2 34.2 %copy-start.35 = (f32[3,256]{1,0:T(4,128)S(1)}, f32[3,256]{1,0:T(4,128)}, u32[]{:S(2)}) copy-start(f32[3,256]{1,0:T(4,128)} %param.51) | copy-start | bytes 9220
  939.8 185.2 %copy-start.32 = (f32[256,1]{0,1:T(1,128)}, f32[256,1]{0,1:T(1,128)S(1)}, u32[]{:S(2)}) copy-start(f32[256,1]{0,1:T(1,128)S(1)} %get-tuple-element.218) | copy-start | bytes 3076
  939.8 185.2 %copy-start.33 = (f32[256,1]{0,1:T(1,128)}, f32[256,1]{0,1:T(1,128)S(1)}, u32[]{:S(2)}) copy-start(f32[256,1]{0,1:T(1,128)S(1)} %get-tuple-element.219) | copy-start | bytes 3076
  (27 other events, 235.9 us)
Sparse Core Ops, SparseCore 0:
  10.2 27.7 all-gather.11
  40.2 31.7 all-gather.17
  74.3 30.3 all-gather.21
  106.7 31.9 all-gather.25
  140.3 68.7 all-gather.13
  210.9 35.1 all-gather.15
  247.9 96.0 all-gather.19
  345.8 96.0 all-gather.23
  443.8 96.1 all-gather.27
  560.4 95.0 reduce-scatter.5
  658.6 238.7 reduce-scatter.3
  900.5 22.8 reduce-scatter.7
  925.9 190.4 all-reduce.2
where the time goes:
time: 1170 us
  waiting for transfers between devices  895 us (76%)
  matrix products  93.1 us (8%)
  other arithmetic  59.4 us (5%)
  blocking collectives  56 us (5%)
  local copies, waits for them, and re-layouts  49.4 us (4%)
  between operations  14.6 us (1%)
    reduce_scatter x1, waiting for transfers between devices, local(): lax.psum_scatter(wide_terms.astype(jnp.bfloat16), 'own', scatter_dimensio...  242 us
    psum x1, waiting for transfers between devices, local(): lax.psum(shares[0].astype(jnp.bfloat16), 'grp').astype(jnp.float32)  175 us
    all_gather x1, waiting for transfers between devices, local(): lax.all_gather(across[2], 'own', axis=0, tiled=True)  95.3 us
    all_gather x1, waiting for transfers between devices, local(): lax.all_gather(across[4], 'own', axis=0, tiled=True)  86.5 us
    all_gather x1, waiting for transfers between devices, local(): lax.all_gather(across[3], 'own', axis=0, tiled=True)  86.4 us
    all_gather x1, waiting for transfers between devices, local(): lax.all_gather(across[0], 'own', axis=0, tiled=True)  53.3 us
    unnamed x106, local copies, waits for them, and re-layouts  40 us
    all_gather x1, waiting for transfers between devices, local(): lax.all_gather(w_down.astype(jnp.bfloat16), 'grp', axis=1, tiled=True)  33.9 us
  transfers between devices with their start and end apart: 15, of which 13 were waited for; matrix products, arithmetic and copies ran while one was open for 11% of the time, Pallas kernels for 0%

commit v1 on v0

v1 whole, which is shorter than its diff:
```python
import jax
import jax.numpy as jnp
from jax import lax
from jax.sharding import PartitionSpec as P


SEQ_LEN = 2048


eps_norm = 1e-05
eps_adam = 1e-08
beta_one = 0.9
beta_two = 0.95
train_step = 5
rate_matrix = 0.004
rate_vector = 0.1
decay_matrix = 0.1

half = jnp.bfloat16
full = jnp.float32


def exchange(block, k):
    devices = range(lax.axis_size("own"))
    return lax.ppermute(block, "own", [(i, i ^ k) for i in devices])


def gather_own(block):
    places = range(1, lax.axis_size("own"))
    arrived = [exchange(block, k) for k in places]
    return jnp.concatenate([block] + arrived, 0)


def scatter_own(part_of):
    places = range(1, lax.axis_size("own"))
    arrived = []
    for k in places:
        part = part_of(k).astype(half)
        arrived.append(exchange(part, k))
    total = part_of(0)
    for block in arrived:
        total = total + block.astype(full)
    return total


def passed_along(block, distance):
    devices = range(lax.axis_size("grp"))
    route = [(i - distance, i) for i in devices if i - distance in devices]
    return lax.ppermute(block, "grp", route)


def exchange_core(block):
    devices = range(lax.axis_size("grp"))
    return lax.ppermute(block, "grp", [(i, i ^ 1) for i in devices])


class Line:

    def __init__(self, array):
        self.chips = lax.axis_size("grp") // 2
        self.array = array
        self.total = 0.0
        self.arrived = None
        self.step = 1

    def going(self):
        return self.step < self.chips

    def hop(self):
        chips, step = self.chips, self.step
        hops = [(step - 1, step), (chips - step, chips - 1 - step)]
        route = [(2 * a + core, 2 * b + core) for a, b in hops for core in range(2)]
        sent = self.array if step == 1 else self.array + self.arrived
        return lax.ppermute(sent, "grp", route)

    def take(self, arrived):
        self.arrived = arrived
        self.total = self.total + arrived.astype(full)
        self.step += 1

    def sum(self):
        return (self.array.astype(full) + self.total).astype(half)


def tick(lines, beside):
    lines = [line for line in lines if line.going()]
    hops = [line.hop() for line in lines]
    hops, beside = lax.optimization_barrier((hops, beside))
    for line, arrived in zip(lines, hops):
        line.take(arrived)
    return beside


def swap_own(pieces):
    return lax.all_to_all(pieces, "own", 0, 0, tiled=True)


def stream_starts(doc_lengths, seq_len):
    starts = jnp.cumsum(doc_lengths, axis=1) - doc_lengths
    base = (jnp.arange(doc_lengths.shape[0], dtype=jnp.int32) * seq_len)[:, None]
    first = (jnp.arange(doc_lengths.shape[1], dtype=jnp.int32) == 0)[None, :]
    return jnp.where(first, 0, base + starts).reshape(-1)


def since_start(positions, stream):
    below = jnp.where(stream[None, :] <= positions[:, None], stream[None, :], 0)
    return positions - jnp.max(below, axis=1)


def apply_adam(param, first, second, grad, rate, decay):
    first_new = beta_one * first + (1.0 - beta_one) * grad
    second_new = beta_two * second + (1.0 - beta_two) * grad * grad
    first_hat = first_new / (1.0 - beta_one**train_step)
    second_hat = second_new / (1.0 - beta_two**train_step)
    param_new = param - rate * (first_hat / (jnp.sqrt(second_hat) + eps_adam) + decay * param)
    return (param_new, first_new, second_new)


def dot(left, right):
    return jnp.dot(left, right, preferred_element_type=full)


def dot_rows(left, right):
    return lax.dot_general(left, right, (((1,), (1,)), ((), ())), preferred_element_type=full)


def dot_tokens(left, right):
    return lax.dot_general(left, right, (((0,), (0,)), ((), ())), preferred_element_type=full)


def pick(index, blocks):
    total = jnp.zeros_like(blocks[0])
    for place, block in enumerate(blocks):
        total = jnp.where(index == place, block, total)
    return total


def local(
    tokens,
    cotangent,
    doc_lengths,
    w_in,
    w_out,
    w_gate,
    w_up,
    w_down,
    conv_w,
    gain,
    gain_two,
    moment_in,
    moment_out,
    moment_gate,
    moment_up,
    moment_down,
    moment_conv,
    moment_gain,
    moment_gain_two,
    square_in,
    square_out,
    square_gate,
    square_up,
    square_down,
    square_conv,
    square_gain,
    square_gain_two,
):
    groups = lax.axis_size("grp")
    owners = lax.axis_size("own")
    group = lax.axis_index("grp")
    owner = lax.axis_index("own")
    rows, width = tokens.shape
    taps = conv_w.shape[0]
    rim = taps - 1
    channels = width // owners
    sub = width // (groups * owners)
    run = w_gate.shape[1] * groups // owners
    share = groups // owners
    thin = w_out.shape[1]

    def columns_for(matrix, pieces):
        cut = matrix.astype(half).T.reshape(pieces, owners, -1, channels)
        return cut.transpose(1, 0, 2, 3).reshape(owners, -1, channels)

    def rows_for(matrix):
        cut = matrix.astype(half).reshape(share, owners, -1, thin)
        return cut.transpose(1, 2, 0, 3).reshape(owners, -1, channels)

    def columns_from(pieces):
        return pieces.transpose(1, 0, 2).reshape(-1, width)

    def rows_gathered(blocks):
        cut = blocks.reshape(groups, -1, groups, thin)
        return cut.transpose(2, 1, 0, 3).reshape(-1, width)

    small = jnp.concatenate([conv_w, gain[None], gain_two[None]], 0).astype(half)
    small = jnp.broadcast_to(small[None], (owners,) + small.shape)
    small_rows = small.shape[1]
    first = jnp.concatenate([columns_for(w_in, 3), rows_for(w_out), small], 1)
    first = swap_own(first)
    tokens_late, first = lax.optimization_barrier((tokens, first))
    x_half = gather_own(tokens_late)
    split = 3 * sub
    small = first[:, split + sub :].transpose(1, 0, 2).reshape(small_rows, width).astype(full)
    first = lax.all_gather(columns_from(first[:, : split + sub]), "grp", axis=0, tiled=False)
    in_t = first[:, :split].reshape(3 * channels, width)
    out_half = rows_gathered(first[:, split:])
    conv_all = small[:taps].reshape(taps, groups, owners, sub)
    conv_float = lax.dynamic_index_in_dim(conv_all, owner, 2, False).reshape(taps, channels)
    gain_float = small[taps]
    gain_two_float = small[taps + 1]
    second = jnp.concatenate([columns_for(w_gate, 1), columns_for(w_up, 1), rows_for(w_down)], 1)
    piece = run // groups
    second = swap_own(second)
    second = lax.all_gather(columns_from(second), "grp", axis=0, tiled=False)
    gate_t = second[:, :piece].reshape(run, width)
    up_t = second[:, piece : 2 * piece].reshape(run, width)
    down_half = rows_gathered(second[:, 2 * piece :])
    cot_late, x_half = lax.optimization_barrier((cotangent, x_half))
    cot_half = gather_own(cot_late)

    places = [owner ^ k for k in range(owners)]
    stream = stream_starts(doc_lengths, SEQ_LEN)
    line = jnp.arange(rows, dtype=jnp.int32)
    position = jnp.concatenate([(group * owners + place) * rows + line for place in places])
    since = since_start(position, stream).reshape(owners, rows, 1)

    x_all = x_half.astype(full)
    inv_all = lax.rsqrt(jnp.mean(x_all * x_all, axis=1, keepdims=True) + eps_norm)
    normed = (x_all * inv_all * gain_float).astype(half)
    project = dot_rows(normed, in_t)
    b_gate = project[:, :channels].reshape(owners, rows, channels)
    c_gate = project[:, channels : 2 * channels].reshape(owners, rows, channels)
    x_value = project[:, 2 * channels :].reshape(owners, rows, channels)
    gated = b_gate * x_value
    tails = [gated[k, rows - rim :] for k in range(owners)]
    last_tail = pick((owners - 1) ^ owner, tails)
    before_group = passed_along(last_tail, 1)
    before = jnp.stack(
        [
            jnp.where(place == 0, before_group, pick((place - 1) ^ owner, tails))
            for place in places
        ]
    )
    extended = jnp.concatenate([before, gated], 1)

    def moved(tap):
        return extended[:, rim - tap : rim - tap + rows]

    convolved = conv_float[0] * gated
    for tap in range(1, taps):
        convolved = convolved + jnp.where(since >= tap, conv_float[tap] * moved(tap), 0.0)
    mixed = (c_gate * convolved).astype(half)
    x_float = tokens.astype(full)
    middle = x_float + scatter_own(lambda k: dot(mixed[k], out_half))
    inv_two = lax.rsqrt(jnp.mean(middle * middle, axis=1, keepdims=True) + eps_norm)
    normed_two = gather_own((middle * inv_two * gain_two_float).astype(half))
    gate = dot_rows(normed_two, gate_t)
    up = dot_rows(normed_two, up_t)
    sig = jax.nn.sigmoid(gate)
    activated = gate * sig
    hidden = (activated * up).astype(half)
    core = group % 2

    def core_half(array, axis):
        count = array.shape[axis] // 2
        keep = lax.dynamic_slice_in_dim(array, core * count, count, axis)
        send = lax.dynamic_slice_in_dim(array, (1 - core) * count, count, axis)
        return (keep.astype(full) + exchange_core(send).astype(full)).astype(half)

    def owner_blocks(array, axis):
        count = array.shape[axis] // owners
        return [
            lax.dynamic_slice_in_dim(array, (owner ^ k) * count, count, axis)
            for k in range(owners)
        ]

    def to_owner(blocks):
        return [blocks[0]] + [exchange(blocks[k], k) for k in range(1, owners)]

    def both_cores(blocks):
        mine = jnp.stack([pick(place ^ owner, blocks) for place in range(owners)])
        other = exchange_core(mine)
        low = jnp.where(core == 0, mine, other)
        high = jnp.where(core == 0, other, mine)
        return low, high

    def join_columns(halves, count):
        both = jnp.concatenate(halves, 1).reshape(owners, -1, count, channels)
        return both.transpose(1, 0, 2, 3).reshape(-1, channels)

    def join_rows(halves, count):
        both = jnp.concatenate(halves, 2).reshape(owners, share, count, width)
        return both.transpose(1, 0, 2, 3).reshape(-1, width)

    down_part = dot_tokens(hidden, cot_half).astype(half)
    gate, up, down_part = lax.optimization_barrier((gate, up, down_part))
    sig = jax.nn.sigmoid(gate)
    activated = gate * sig
    down_line = Line(core_half(down_part, 1))
    grad_hidden = dot_rows(cot_half, down_half)
    grad_gate = (grad_hidden * up * sig * (1.0 + gate * (1.0 - sig))).astype(half)
    grad_up = (grad_hidden * activated).astype(half)

    def block(array, k):
        return array[k * rows : (k + 1) * rows]

    gate_part = dot_tokens(grad_gate, normed_two).astype(half)
    gate_line = Line(core_half(gate_part, 0))
    up_part = dot_tokens(grad_up, normed_two).astype(half)
    up_line = Line(core_half(up_part, 0))

    grad_normed_two = scatter_own(
        lambda k: dot(block(grad_gate, k), gate_t) + dot(block(grad_up, k), up_t),
    )
    grad_normed_two, gate_line.array = tick([down_line], (grad_normed_two, gate_line.array))
    gain_two_rows = jnp.sum(grad_normed_two * middle * inv_two, axis=0)
    weighted_two = gain_two_float * grad_normed_two
    grad_middle = (
        cotangent.astype(full)
        + inv_two * weighted_two
        - middle
        * inv_two
        * inv_two
        * inv_two
        * jnp.mean(weighted_two * middle, axis=1, keepdims=True)
    )
    grad_middle_half = gather_own(grad_middle.astype(half))
    grad_middle_half, up_line.array, hidden_late = tick(
        [down_line, gate_line], (grad_middle_half, up_line.array, hidden)
    )
    grad_mixed = dot_rows(grad_middle_half, out_half).reshape(owners, rows, channels)
    grad_c = grad_mixed * convolved
    grad_conv = grad_mixed * c_gate
    tap_sums = [jnp.sum(grad_conv * gated, axis=(0, 1))]
    grad_gated = conv_float[0] * grad_conv
    kept = [jnp.where(since >= tap, grad_conv, 0.0) for tap in range(1, taps)]
    heads = [
        jnp.concatenate([kept[tap - 1][k, :tap] for tap in range(1, taps)], 0)
        for k in range(owners)
    ]
    after_group = passed_along(pick(owner, heads), -1)
    after = jnp.stack(
        [
            jnp.where(place == owners - 1, after_group, pick((place + 1) ^ owner, heads))
            for place in places
        ]
    )
    line = 0
    for tap in range(1, taps):
        ahead = jnp.concatenate([kept[tap - 1][:, tap:], after[:, line : line + tap]], 1)
        line = line + tap
        grad_gated = grad_gated + conv_float[tap] * ahead
        tap_sums.append(jnp.sum(kept[tap - 1] * moved(tap), axis=(0, 1)))
    grad_project = (
        jnp.concatenate([grad_gated * x_value, grad_c, grad_gated * b_gate], 2)
        .astype(half)
        .reshape(owners * rows, 3 * channels)
    )
    in_part = core_half(dot_tokens(grad_project, normed).astype(half), 0)
    out_part = core_half(
        dot_tokens(mixed.reshape(owners * rows, channels), grad_middle_half).astype(half), 1
    )
    in_rows, out_rows = in_part.shape[0], out_part.shape[0] // 2
    out_part = jnp.concatenate([out_part[:out_rows], out_part[out_rows:]], 1)
    last_line = Line(jnp.concatenate([in_part, out_part], 0))
    feed_out = scatter_own(lambda k: dot(block(hidden_late, k), down_half))
    block_out = (middle + feed_out).astype(half)
    last_line.array, block_out, project_late = tick(
        [down_line, gate_line, up_line], (last_line.array, block_out, grad_project)
    )
    grad_normed = scatter_own(lambda k: dot(block(project_late, k), in_t))

    piece = run // groups
    while down_line.going():
        tick([down_line, gate_line, up_line, last_line], ())
    down_blocks = to_owner(owner_blocks(down_line.sum(), 0))
    down_blocks = tick([gate_line, up_line, last_line], down_blocks)
    gate_blocks = to_owner(owner_blocks(gate_line.sum(), 1))
    down_grad = join_rows(both_cores(down_blocks), piece)
    gate_blocks, down_grad, grad_normed = tick(
        [up_line, last_line], (gate_blocks, down_grad, grad_normed)
    )
    inv_rms = lax.rsqrt(jnp.mean(x_float * x_float, axis=1, keepdims=True) + eps_norm)
    gain_rows = jnp.sum(grad_normed * x_float * inv_rms, axis=0)
    weighted = gain_float * grad_normed
    grad_tokens = (
        grad_middle
        + inv_rms * weighted
        - x_float
        * inv_rms
        * inv_rms
        * inv_rms
        * jnp.mean(weighted * x_float, axis=1, keepdims=True)
    ).astype(half)
    tap_pieces = jnp.stack(tap_sums).reshape(taps, owners, share * sub).transpose(1, 0, 2)
    tap_pieces = jnp.pad(tap_pieces, ((0, 0), (0, 0), (0, channels - share * sub)))
    gain_pieces = jnp.stack([gain_rows, gain_two_rows]).reshape(2, owners, channels)
    pieces = jnp.concatenate([tap_pieces, gain_pieces.transpose(1, 0, 2)], 1)
    pieces = swap_own(pieces)
    tap_share = pieces[:, :taps, : share * sub].reshape(owners, taps, share, sub)
    tap_share = tap_share.transpose(1, 2, 0, 3).reshape(taps, channels)
    gain_share = jnp.sum(pieces[:, taps:], axis=0)
    small_share = jnp.concatenate([tap_share, gain_share], 0)

    up_blocks = to_owner(owner_blocks(up_line.sum(), 1))
    gate_grad = join_columns(both_cores(gate_blocks), piece)
    down_shard = lax.dynamic_slice_in_dim(down_grad, group * thin, thin, 1)
    down_new = apply_adam(
        w_down, moment_down, square_down, down_shard.astype(full), rate_matrix, decay_matrix
    )
    up_blocks, gate_grad, down_grad, down_new, grad_tokens, small_share = tick(
        [last_line],
        (up_blocks, gate_grad, down_grad.astype(full), down_new, grad_tokens, small_share),
    )
    up_grad = join_columns(both_cores(up_blocks), piece)
    last = last_line.sum()
    out_sum = jnp.concatenate([last[in_rows:, : width // 2], last[in_rows:, width // 2 :]], 0)
    last_blocks = [
        jnp.concatenate([wide] + jnp.split(rest, owners // 2, 1), 0)
        for wide, rest in zip(owner_blocks(last[:in_rows], 1), owner_blocks(out_sum, 0))
    ]
    last_halves = both_cores(to_owner(last_blocks))
    in_halves = [part[:, :in_rows] for part in last_halves]
    out_halves = [
        jnp.concatenate(jnp.split(part[:, in_rows:], owners // 2, 1), 2) for part in last_halves
    ]
    out_grad = join_rows(out_halves, sub)
    in_grad = join_columns(in_halves, sub)
    grad_w_down = down_grad
    grad_w_out = out_grad.astype(full)

    def turned(grad_t):
        return lax.optimization_barrier(grad_t.T)

    def my_rows(grad_t):
        count = grad_t.shape[0] // groups
        return turned(lax.dynamic_slice_in_dim(grad_t, group * count, count, 0))

    grad_w_gate = turned(gate_grad).astype(full)
    grad_w_up = turned(up_grad).astype(full)
    grad_w_in = turned(in_grad).astype(full)

    out_shard = lax.dynamic_slice_in_dim(out_grad, group * thin, thin, 1)
    gate_shard = my_rows(gate_grad)
    up_shard = my_rows(up_grad)
    in_shard = my_rows(in_grad)

    for bit in range(groups.bit_length() - 1):
        route = [(i, i ^ (1 << bit)) for i in range(groups)]
        small_share = small_share + lax.ppermute(small_share, "grp", route)
    grad_conv_w = small_share[:taps]
    grad_gain = small_share[taps]
    grad_gain_two = small_share[taps + 1]

    new_w_in, new_moment_in, new_square_in = apply_adam(
        w_in, moment_in, square_in, in_shard.astype(full), rate_matrix, decay_matrix
    )
    new_w_out, new_moment_out, new_square_out = apply_adam(
        w_out, moment_out, square_out, out_shard.astype(full), rate_matrix, decay_matrix
    )
    new_w_gate, new_moment_gate, new_square_gate = apply_adam(
        w_gate, moment_gate, square_gate, gate_shard.astype(full), rate_matrix, decay_matrix
    )
    new_w_up, new_moment_up, new_square_up = apply_adam(
        w_up, moment_up, square_up, up_shard.astype(full), rate_matrix, decay_matrix
    )
    new_w_down, new_moment_down, new_square_down = down_new
    new_conv_w, new_moment_conv, new_square_conv = apply_adam(
        conv_w, moment_conv, square_conv, grad_conv_w, rate_vector, 0.0
    )
    new_gain, new_moment_gain, new_square_gain = apply_adam(
        gain, moment_gain, square_gain, grad_gain, rate_vector, 0.0
    )
    new_gain_two, new_moment_gain_two, new_square_gain_two = apply_adam(
        gain_two, moment_gain_two, square_gain_two, grad_gain_two, rate_vector, 0.0
    )
    return (
        block_out,
        grad_tokens,
        grad_w_in,
        grad_w_out,
        grad_w_gate,
        grad_w_up,
        grad_w_down,
        grad_conv_w,
        grad_gain,
        grad_gain_two,
        new_w_in,
        new_w_out,
        new_w_gate,
        new_w_up,
        new_w_down,
        new_conv_w,
        new_gain,
        new_gain_two,
        new_moment_in,
        new_moment_out,
        new_moment_gate,
        new_moment_up,
        new_moment_down,
        new_moment_conv,
        new_moment_gain,
        new_moment_gain_two,
        new_square_in,
        new_square_out,
        new_square_gate,
        new_square_up,
        new_square_down,
        new_square_conv,
        new_square_gain,
        new_square_gain_two,
    )


def solution(mesh):
    placed = (
        P(("grp", "own"), None),
        P(("grp", "own"), None),
        P(),
        P("own", "grp"),
        P("own", "grp"),
        P("own", "grp"),
        P("own", "grp"),
        P("own", "grp"),
        P(None, "own"),
        P("own"),
        P("own"),
        P("own", "grp"),
        P("own", "grp"),
        P("own", "grp"),
        P("own", "grp"),
        P("own", "grp"),
        P(None, "own"),
        P("own"),
        P("own"),
        P("own", "grp"),
        P("own", "grp"),
        P("own", "grp"),
        P("own", "grp"),
        P("own", "grp"),
        P(None, "own"),
        P("own"),
        P("own"),
    )

    return jax.shard_map(
        local,
        mesh=mesh,
        in_specs=placed,
        out_specs=(
            P(("grp", "own"), None),
            P(("grp", "own"), None),
            P("own", None),
            P("own", None),
            P("own", None),
            P("own", None),
            P("own", None),
            P(None, "own"),
            P("own"),
            P("own"),
            P("own", "grp"),
            P("own", "grp"),
            P("own", "grp"),
            P("own", "grp"),
            P("own", "grp"),
            P(None, "own"),
            P("own"),
            P("own"),
            P("own", "grp"),
            P("own", "grp"),
            P("own", "grp"),
            P("own", "grp"),
            P("own", "grp"),
            P(None, "own"),
            P("own"),
            P("own"),
            P("own", "grp"),
            P("own", "grp"),
            P("own", "grp"),
            P("own", "grp"),
            P("own", "grp"),
            P(None, "own"),
            P("own"),
            P("own"),
        ),
        check_vma=False,
    )
```

time: 1170 us -> 491 us (0.42)
  waiting for transfers between devices: 895 us -> 156 us
  starting transfers between devices: 5.93 us -> 92.7 us
  blocking collectives: 56 us -> 25.3 us
  matrix products: 93.1 us -> 63.4 us
  other arithmetic: 59.4 us -> 80.9 us
    all_gather x9 -> x2, waiting for transfers between devices: 449 us -> 7.49 us  [the longest x1 7.47 us: local(): second = lax.all_gather(columns_from(second), 'grp', axis=0, tiled=False)]
    reduce_scatter x3 -> x0, waiting for transfers between devices: 271 us -> none  [the longest x1 242 us: local(): lax.psum_scatter(wide_terms.astype(jnp.bfloat16), 'own', scatter_dimensio...]
    psum x1 -> x0, waiting for transfers between devices: 175 us -> none  [local(): lax.psum(shares[0].astype(jnp.bfloat16), 'grp').astype(jnp.float32)]
    ppermute x2 -> x62, waiting for transfers between devices: 0.01 us -> 149 us  [the longest x36 99 us: exchange(): return lax.ppermute(block, 'own', [(i, i ^ k) for i in devices])]
    ppermute x2 -> x62, starting transfers between devices: 4.93 us -> 89.4 us  [the longest x36 42.5 us: exchange(): return lax.ppermute(block, 'own', [(i, i ^ k) for i in devices])]
    all_gather x4 -> x0, blocking collectives: 39.7 us -> none  [the longest x1 14.9 us: local(): lax.all_gather(w_out.astype(jnp.bfloat16), 'grp', axis=1, tiled=True)]
    dot_general x15 -> x30, matrix products: 93.1 us -> 63.4 us  [the longest x20 26.5 us: dot(): return jnp.dot(left, right, preferred_element_type=full)]
    all_to_all x0 -> x2, blocking collectives: none -> 25.3 us  [swap_own(): return lax.all_to_all(pieces, 'own', 0, 0, tiled=True)]
  transfers between devices with their start and end apart: 15 -> 65, of which waited for: 13 -> 28; matrix products, arithmetic and copies ran while one was open for 11% -> 26% of each run, Pallas kernels for 0% -> 0%
where the time goes in v1:
time: 491 us; the launch traced here: 483 us
  waiting for transfers between devices  156 us (32%)
  starting transfers between devices  92.7 us (19%)
  other arithmetic  80.9 us (16%)
  matrix products  63.4 us (13%)
  local copies, waits for them, and re-layouts  47.7 us (10%)
  blocking collectives  25.3 us (5%)
  between operations  16.7 us (3%)
    ppermute x36, waiting for transfers between devices, exchange(): return lax.ppermute(block, 'own', [(i, i ^ k) for i in devices])  99 us
    ppermute x12, waiting for transfers between devices, hop(): return lax.ppermute(sent, 'grp', route)  45.9 us
    ppermute x36, starting transfers between devices, exchange(): return lax.ppermute(block, 'own', [(i, i ^ k) for i in devices])  42.5 us
    ppermute x12, starting transfers between devices, hop(): return lax.ppermute(sent, 'grp', route)  36.3 us
    unnamed x230, local copies, waits for them, and re-layouts  26.9 us
    dot_general x20, matrix products, dot(): return jnp.dot(left, right, preferred_element_type=full)  26.5 us
    all_to_all x2, blocking collectives, swap_own(): return lax.all_to_all(pieces, 'own', 0, 0, tiled=True)  25.3 us
    dot_general x5, matrix products, dot_rows(): lax.dot_general(left, right, (((1,), (1,)), ((), ())), preferred_element_...  21.3 us
  transfers between devices with their start and end apart: 65, of which 28 were waited for; matrix products, arithmetic and copies ran while one was open for 26% of the time, Pallas kernels for 0%

profile of v1, /device:TPU:0, one launch (start us, length us, event | category | flops | bytes accessed | tf_op | source)
XLA Modules:
  0.0 483.1 jit_solution(2650187308738811125)
XLA Ops:
  11.9 11.3 %all_to_all.15 = bf16[4,133,256]{2,1,0:T(8,128)(2,1)S(1)} all-to-all(bf16[4,133,256]{2,1,0:T(8,128)(2,1)S(1)} %pad_maximum_fusion.18), channel_id=1, replica_groups=mesh['grp'=8,'own'=4] {'own'}, dimensions={0} | all-to-all | bytes 544768 | tf_op jit(solution)/shard_map/all_to_all | solution.py:95
  25.0 14.0 %all_to_all.16 = bf16[4,432,256]{2,1,0:T(8,128)(2,1)S(1)} all-to-all(bf16[4,432,256]{2,1,0:T(8,128)(2,1)S(1)} %pad_maximum_fusion.16), channel_id=1, replica_groups=mesh['grp'=8,'own'=4] {'own'}, dimensions={0} | all-to-all | bytes 1769472 | tf_op jit(solution)/shard_map/all_to_all | solution.py:95
  45.6 10.9 %collective-permute-done = bf16[256,1024]{1,0:T(8,128)(2,1)S(1)} collective-permute-done((bf16[256,1024]{1,0:T(8,128)(2,1)S(1)}, bf16[256,1024]{1,0:T(8,128)(2,1)S(1)}, u32[]{:S(2)}, u32[]{:S(2)}) %collective-permute-start) | collective-permute-done | bytes 524320 | tf_op jit(solution)/shard_map/ppermute | solution.py:25
  56.5 8.7 %collective-permute-done.1 = bf16[256,1024]{1,0:T(8,128)(2,1)S(1)} collective-permute-done((bf16[256,1024]{1,0:T(8,128)(2,1)S(1)}, bf16[256,1024]{1,0:T(8,128)(2,1)S(1)}, u32[]{:S(2)}, u32[]{:S(2)}) %collective-permute-start.1) | collective-permute-done | bytes 524320 | tf_op jit(solution)/shard_map/ppermute | solution.py:25
  89.3 5.2 %collective-permute-done.4 = bf16[256,1024]{1,0:T(8,128)(2,1)} collective-permute-done((bf16[256,1024]{1,0:T(8,128)(2,1)}, bf16[256,1024]{1,0:T(8,128)(2,1)}, u32[]{:S(2)}, u32[]{:S(2)}) %collective-permute-start.4) | collective-permute-done | bytes 524320 | tf_op jit(solution)/shard_map/ppermute | solution.py:25
  96.1 10.3 %collective-permute-done.6 = bf16[256,1024]{1,0:T(8,128)(2,1)} collective-permute-done((bf16[256,1024]{1,0:T(8,128)(2,1)}, bf16[256,1024]{1,0:T(8,128)(2,1)}, u32[]{:S(2)}, u32[]{:S(2)}) %collective-permute-start.6) | collective-permute-done | bytes 524320 | tf_op jit(solution)/shard_map/ppermute | solution.py:25
  112.2 5.4 %collective-permute-done.12 = bf16[256,1024]{1,0:T(8,128)(2,1)S(1)} collective-permute-done((bf16[256,1024]{1,0:T(8,128)(2,1)}, bf16[256,1024]{1,0:T(8,128)(2,1)S(1)}, u32[]{:S(2)}, u32[]{:S(2)}) %collective-permute-start.12) | collective-permute-done | bytes 524320 | tf_op jit(solution)/shard_map/ppermute | solution.py:25
  118.3 7.5 %all-gather.5.cloned.1.call-done = bf16[8,432,1024]{2,1,0:T(8,128)(2,1)} async-done(((bf16[1,432,1024]{2,1,0:T(8,128)(2,1)}), bf16[8,432,1024]{2,1,0:T(8,128)(2,1)}) %all-gather.5.cloned.1.call-update) | async-done | bytes 7077904 | tf_op jit(solution)/shard_map/all_gather | solution.py:214
  125.8 4.0 fusion.139
  129.8 5.1 %collective-permute-done.9 = bf16[256,1024]{1,0:T(8,128)(2,1)} collective-permute-done((bf16[256,1024]{1,0:T(8,128)(2,1)S(1)}, bf16[256,1024]{1,0:T(8,128)(2,1)}, u32[]{:S(2)}, u32[]{:S(2)}) %collective-permute-start.9) | collective-permute-done | bytes 524320 | tf_op jit(solution)/shard_map/ppermute | solution.py:25
  134.9 4.1 fusion.124
  139.1 6.5 %multiply_convert_fusion.2 = (bf16[1024,1152]{1,0:T(8,128)(2,1)S(1)}, f32[1024,1152]{1,0:T(8,128)}) fusion(f32[1024,1152]{1,0:T(8,128)S(1)} %fusion.124, bf16[1152,1024]{1,0:T(8,128)(2,1)S(1)} %bitcast.264, bf16[256,1024]{1,0:T(8,128)(2,1)} %collective-permute-done.9, bf16[256,1024]{1,0:T(8,128)(2,1)} %collective-permute-done.8, ...), kind=kOutput, calls=%fused_computation.5 | convolution fusion | flops 2431385600 | bytes 16252928 | tf_op jit(solution)/shard_map/dot_general | solution.py:124
  145.6 5.1 %convolution_convert_fusion.2 = bf16[1152,1024]{1,0:T(8,128)(2,1)S(1)} fusion(bf16[1024,1152]{1,0:T(8,128)(2,1)S(1)} %get-tuple-element.96, bf16[1024,1024]{1,0:T(8,128)(2,1)} %constant_dynamic-update-slice_fusion), kind=kOutput, calls=%fused_computation.11 | convolution fusion | flops 2417098752 | bytes 6815744 | tf_op jit(solution)/shard_map/dot_general | solution.py:128
  152.9 8.1 %multiply_convert_fusion = (bf16[1024,1152]{1,0:T(8,128)(2,1)S(1)}, bf16[1024,1152]{1,0:T(8,128)(2,1)S(1)}) fusion(f32[1024,1152]{1,0:T(8,128)S(1)} %fusion.124, f32[1024,1152]{1,0:T(8,128)} %get-tuple-element.87, bf16[1024,1024]{1,0:T(8,128)(2,1)} %constant_dynamic-update-slice_fusion, bf16[144,8,8,128]{3,2,1,0:T(8,128)(2,1)S(1)} %bitcast.306), kind=kOutput, calls=%fused_computation.2 | convolution fusion | flops 2431254528 | bytes 18612224 | tf_op jit(solution)/shard_map/dot_general | solution.py:124
  162.2 3.9 convolution_convert_fusion.1
  166.2 6.5 %collective-permute-start.18 = (bf16[576,1024]{1,0:T(8,128)(2,1)S(1)}, bf16[576,1024]{1,0:T(8,128)(2,1)S(1)}, u32[]{:S(2)}, u32[]{:S(2)}) collective-permute-start(bf16[576,1024]{1,0:T(8,128)(2,1)S(1)} %constant_dynamic-slice_fusion.21), channel_id=1, source_target_pairs={{0,4},{4,0},{8,12},{12,8},{16,20},{20,16},{24,28},{28,24},{1,5},{5... | collective-permute-start | bytes 3538952 | tf_op jit(solution)/shard_map/ppermute | solution.py:54
  181.4 6.1 %collective-permute-start.14 = (bf16[1152,512]{1,0:T(8,128)(2,1)S(1)}, bf16[1152,512]{1,0:T(8,128)(2,1)S(1)}, u32[]{:S(2)}, u32[]{:S(2)}) collective-permute-start(bf16[1152,512]{1,0:T(8,128)(2,1)S(1)} %add_convert_fusion.5), channel_id=1, source_target_pairs={{0,8},{4,12},{24,16},{28,20},{1,9},{5,13},{25,17},{29,21},{2,10},{... | collective-permute-start | bytes 3538952 | tf_op jit(solution)/shard_map/ppermute | solution.py:74
  187.5 3.8 convolution_convert_fusion
  192.8 9.8 %collective-permute-done.16 = bf16[256,1024]{1,0:T(8,128)(2,1)S(1)} collective-permute-done((bf16[256,1024]{1,0:T(8,128)(2,1)S(1)}, bf16[256,1024]{1,0:T(8,128)(2,1)S(1)}, u32[]{:S(2)}, u32[]{:S(2)}) %collective-permute-start.16) | collective-permute-done | bytes 524320 | tf_op jit(solution)/shard_map/ppermute | solution.py:25
  204.1 8.0 %collective-permute-done.14 = bf16[1152,512]{1,0:T(8,128)(2,1)S(1)} collective-permute-done((bf16[1152,512]{1,0:T(8,128)(2,1)S(1)}, bf16[1152,512]{1,0:T(8,128)(2,1)S(1)}, u32[]{:S(2)}, u32[]{:S(2)}) %collective-permute-start.14) | collective-permute-done | bytes 1179680 | tf_op jit(solution)/shard_map/ppermute | solution.py:74
  215.3 7.1 %collective-permute-start.20 = (bf16[576,1024]{1,0:T(8,128)(2,1)S(1)}, bf16[576,1024]{1,0:T(8,128)(2,1)}, u32[]{:S(2)}, u32[]{:S(2)}) collective-permute-start(bf16[576,1024]{1,0:T(8,128)(2,1)S(1)} %add_convert_fusion.4), channel_id=1, source_target_pairs={{0,8},{4,12},{24,16},{28,20},{1,9},{5,13},{25,17},{29,21},{2,10},{... | collective-permute-start | bytes 3538952 | tf_op jit(solution)/shard_map/ppermute | solution.py:74
  233.7 6.4 %collective-permute-done.21 = bf16[256,1024]{1,0:T(8,128)(2,1)} collective-permute-done((bf16[256,1024]{1,0:T(8,128)(2,1)}, bf16[256,1024]{1,0:T(8,128)(2,1)}, u32[]{:S(2)}, u32[]{:S(2)}) %collective-permute-start.21) | collective-permute-done | bytes 524320 | tf_op jit(solution)/shard_map/ppermute | solution.py:25
  240.2 9.4 %collective-permute-done.23 = bf16[256,1024]{1,0:T(8,128)(2,1)} collective-permute-done((bf16[256,1024]{1,0:T(8,128)(2,1)}, bf16[256,1024]{1,0:T(8,128)(2,1)}, u32[]{:S(2)}, u32[]{:S(2)}) %collective-permute-start.23) | collective-permute-done | bytes 524320 | tf_op jit(solution)/shard_map/ppermute | solution.py:25
  274.4 4.7 collective-permute-start.27
  279.1 6.3 %collective-permute-done.32 = bf16[256,1024]{1,0:T(8,128)(2,1)S(1)} collective-permute-done((bf16[256,1024]{1,0:T(8,128)(2,1)S(1)}, bf16[256,1024]{1,0:T(8,128)(2,1)S(1)}, u32[]{:S(2)}, u32[]{:S(2)}) %collective-permute-start.32) | collective-permute-done | bytes 524320 | tf_op jit(solution)/shard_map/ppermute | solution.py:25
  288.1 15.0 %collective-permute-done.25 = bf16[1152,512]{1,0:T(8,128)(2,1)S(1)} collective-permute-done((bf16[1152,512]{1,0:T(8,128)(2,1)S(1)}, bf16[1152,512]{1,0:T(8,128)(2,1)S(1)}, u32[]{:S(2)}, u32[]{:S(2)}) %collective-permute-start.25) | collective-permute-done | bytes 1179680 | tf_op jit(solution)/shard_map/ppermute | solution.py:74
  312.5 7.6 %collective-permute-start.36 = (bf16[512,1024]{1,0:T(8,128)(2,1)S(1)}, bf16[512,1024]{1,0:T(8,128)(2,1)}, u32[]{:S(2)}, u32[]{:S(2)}) collective-permute-start(bf16[512,1024]{1,0:T(8,128)(2,1)S(1)} %maximum_maximum_fusion), channel_id=1, source_target_pairs={{0,8},{4,12},{24,16},{28,20},{1,9},{5,13},{25,17},{29,21},{2,10},{... | collective-permute-start | bytes 3145736 | tf_op jit(solution)/shard_map/ppermute | solution.py:74
  336.4 4.7 collective-permute-done.38
  356.2 6.6 %collective-permute-done.47 = bf16[256,1024]{1,0:T(8,128)(2,1)} collective-permute-done((bf16[256,1024]{1,0:T(8,128)(2,1)}, bf16[256,1024]{1,0:T(8,128)(2,1)}, u32[]{:S(2)}, u32[]{:S(2)}) %collective-permute-start.47) | collective-permute-done | bytes 524320 | tf_op jit(solution)/shard_map/ppermute | solution.py:25
  375.4 3.7 collective-permute-done.43
  379.1 4.4 collective-permute-done.40
  413.4 17.2 %collective-permute-done.49 = bf16[512,1024]{1,0:T(8,128)(2,1)} collective-permute-done((bf16[512,1024]{1,0:T(8,128)(2,1)}, bf16[512,1024]{1,0:T(8,128)(2,1)}, u32[]{:S(2)}, u32[]{:S(2)}) %collective-permute-start.49) | collective-permute-done | bytes 1048608 | tf_op jit(solution)/shard_map/ppermute | solution.py:74
  (550 shorter events, 229.0 us)
Async XLA Ops:
  7.2 60.8 %all-gather.3.cloned.1.call-start = ((), (), s32[]{:S(2)}) async-start(), calls=%async_computation.3 | async-start | bytes 2359296 | tf_op jit(solution)/shard_map/all_gather | solution.py:204
  24.3 101.6 %all-gather.5.cloned.1.call-start = ((), (), s32[]{:S(2)}) async-start(), calls=%async_computation.4 | async-start | bytes 7962624 | tf_op jit(solution)/shard_map/all_gather | solution.py:214
  42.5 22.7 %collective-permute-start.1 = (bf16[256,1024]{1,0:T(8,128)(2,1)S(1)}, bf16[256,1024]{1,0:T(8,128)(2,1)S(1)}, u32[]{:S(2)}, u32[]{:S(2)}) collective-permute-start(bf16[256,1024]{1,0:T(8,128)(2,1)S(1)} %copy-done.11), channel_id=1, source_target_pairs={{0,2},{1,3},{2,0},{3,1},{4,6},{5,7},{6,4},{7,5},{8,10},{9,11},{10,... | collective-permute-start | bytes 1572872 | tf_op jit(solution)/shard_map/ppermute | solution.py:25
  43.1 22.2 %collective-permute-start.2 = (bf16[256,1024]{1,0:T(8,128)(2,1)S(1)}, bf16[256,1024]{1,0:T(8,128)(2,1)S(1)}, u32[]{:S(2)}, u32[]{:S(2)}) collective-permute-start(bf16[256,1024]{1,0:T(8,128)(2,1)S(1)} %copy-done.11), channel_id=1, source_target_pairs={{0,3},{1,2},{2,1},{3,0},{4,7},{5,6},{6,5},{7,4},{8,11},{9,10},{10,... | collective-permute-start | bytes 1572872 | tf_op jit(solution)/shard_map/ppermute | solution.py:25
  65.4 20.7 %collective-permute-start.10 = (bf16[256,1024]{1,0:T(8,128)(2,1)}, bf16[256,1024]{1,0:T(8,128)(2,1)S(1)}, u32[]{:S(2)}, u32[]{:S(2)}) collective-permute-start(bf16[256,1024]{1,0:T(8,128)(2,1)} %param.28), channel_id=1, source_target_pairs={{0,1},{1,0},{2,3},{3,2},{4,5},{5,4},{6,7},{7,6},{8,9},{9,8},{10,11... | collective-permute-start | bytes 1572872 | tf_op jit(solution)/shard_map/ppermute | solution.py:25
  66.4 22.1 %collective-permute-start.11 = (bf16[256,1024]{1,0:T(8,128)(2,1)}, bf16[256,1024]{1,0:T(8,128)(2,1)S(1)}, u32[]{:S(2)}, u32[]{:S(2)}) collective-permute-start(bf16[256,1024]{1,0:T(8,128)(2,1)} %param.28), channel_id=1, source_target_pairs={{0,2},{1,3},{2,0},{3,1},{4,6},{5,7},{6,4},{7,5},{8,10},{9,11},{10,... | collective-permute-start | bytes 1572872 | tf_op jit(solution)/shard_map/ppermute | solution.py:25
  82.8 23.5 %collective-permute-start.6 = (bf16[256,1024]{1,0:T(8,128)(2,1)}, bf16[256,1024]{1,0:T(8,128)(2,1)}, u32[]{:S(2)}, u32[]{:S(2)}) collective-permute-start(bf16[256,1024]{1,0:T(8,128)(2,1)} %convolution_convert_fusion.4), channel_id=1, source_target_pairs={{0,3},{1,2},{2,1},{3,0},{4,7},{5,6},{6,5},{7,4},{8,11},{9,10},{10,... | collective-permute-start | bytes 1572872 | tf_op jit(solution)/shard_map/ppermute | solution.py:25
  86.1 31.4 %collective-permute-start.12 = (bf16[256,1024]{1,0:T(8,128)(2,1)}, bf16[256,1024]{1,0:T(8,128)(2,1)S(1)}, u32[]{:S(2)}, u32[]{:S(2)}) collective-permute-start(bf16[256,1024]{1,0:T(8,128)(2,1)} %param.28), channel_id=1, source_target_pairs={{0,3},{1,2},{2,1},{3,0},{4,7},{5,6},{6,5},{7,4},{8,11},{9,10},{10,... | collective-permute-start | bytes 1572872 | tf_op jit(solution)/shard_map/ppermute | solution.py:25
  108.6 21.2 %collective-permute-start.7 = (bf16[256,1024]{1,0:T(8,128)(2,1)S(1)}, bf16[256,1024]{1,0:T(8,128)(2,1)S(1)}, u32[]{:S(2)}, u32[]{:S(2)}) collective-permute-start(bf16[256,1024]{1,0:T(8,128)(2,1)S(1)} %multiply_convert_fusion.6), channel_id=1, source_target_pairs={{0,1},{1,0},{2,3},{3,2},{4,5},{5,4},{6,7},{7,6},{8,9},{9,8},{10,11... | collective-permute-start | bytes 1572872 | tf_op jit(solution)/shard_map/ppermute | solution.py:25
  110.4 24.6 %collective-permute-start.9 = (bf16[256,1024]{1,0:T(8,128)(2,1)S(1)}, bf16[256,1024]{1,0:T(8,128)(2,1)}, u32[]{:S(2)}, u32[]{:S(2)}) collective-permute-start(bf16[256,1024]{1,0:T(8,128)(2,1)S(1)} %multiply_convert_fusion.6), channel_id=1, source_target_pairs={{0,3},{1,2},{2,1},{3,0},{4,7},{5,6},{6,5},{7,4},{8,11},{9,10},{10,... | collective-permute-start | bytes 1572872 | tf_op jit(solution)/shard_map/ppermute | solution.py:25
  166.2 37.4 %collective-permute-start.18 = (bf16[576,1024]{1,0:T(8,128)(2,1)S(1)}, bf16[576,1024]{1,0:T(8,128)(2,1)S(1)}, u32[]{:S(2)}, u32[]{:S(2)}) collective-permute-start(bf16[576,1024]{1,0:T(8,128)(2,1)S(1)} %constant_dynamic-slice_fusion.21), channel_id=1, source_target_pairs={{0,4},{4,0},{8,12},{12,8},{16,20},{20,16},{24,28},{28,24},{1,5},{5... | collective-permute-start | bytes 3538952 | tf_op jit(solution)/shard_map/ppermute | solution.py:54
  176.9 25.6 %collective-permute-start.16 = (bf16[256,1024]{1,0:T(8,128)(2,1)S(1)}, bf16[256,1024]{1,0:T(8,128)(2,1)S(1)}, u32[]{:S(2)}, u32[]{:S(2)}) collective-permute-start(bf16[256,1024]{1,0:T(8,128)(2,1)S(1)} %fusion.40), channel_id=1, source_target_pairs={{0,2},{1,3},{2,0},{3,1},{4,6},{5,7},{6,4},{7,5},{8,10},{9,11},{10,... | collective-permute-start | bytes 1572872 | tf_op jit(solution)/shard_map/ppermute | solution.py:25
  179.7 22.9 %collective-permute-start.17 = (bf16[256,1024]{1,0:T(8,128)(2,1)S(1)}, bf16[256,1024]{1,0:T(8,128)(2,1)S(1)}, u32[]{:S(2)}, u32[]{:S(2)}) collective-permute-start(bf16[256,1024]{1,0:T(8,128)(2,1)S(1)} %fusion.41), channel_id=1, source_target_pairs={{0,3},{1,2},{2,1},{3,0},{4,7},{5,6},{6,5},{7,4},{8,11},{9,10},{10,... | collective-permute-start | bytes 1572872 | tf_op jit(solution)/shard_map/ppermute | solution.py:25
  181.4 30.7 %collective-permute-start.14 = (bf16[1152,512]{1,0:T(8,128)(2,1)S(1)}, bf16[1152,512]{1,0:T(8,128)(2,1)S(1)}, u32[]{:S(2)}, u32[]{:S(2)}) collective-permute-start(bf16[1152,512]{1,0:T(8,128)(2,1)S(1)} %add_convert_fusion.5), channel_id=1, source_target_pairs={{0,8},{4,12},{24,16},{28,20},{1,9},{5,13},{25,17},{29,21},{2,10},{... | collective-permute-start | bytes 3538952 | tf_op jit(solution)/shard_map/ppermute | solution.py:74
  192.7 34.0 %collective-permute-start.24 = (bf16[576,1024]{1,0:T(8,128)(2,1)S(1)}, bf16[576,1024]{1,0:T(8,128)(2,1)S(1)}, u32[]{:S(2)}, u32[]{:S(2)}) collective-permute-start(bf16[576,1024]{1,0:T(8,128)(2,1)S(1)} %constant_dynamic-slice_fusion.20), channel_id=1, source_target_pairs={{0,4},{4,0},{8,12},{12,8},{16,20},{20,16},{24,28},{28,24},{1,5},{5... | collective-permute-start | bytes 3538952 | tf_op jit(solution)/shard_map/ppermute | solution.py:54
  213.6 37.7 %collective-permute-start.19 = (bf16[1152,512]{1,0:T(8,128)(2,1)}, bf16[1152,512]{1,0:T(8,128)(2,1)}, u32[]{:S(2)}, u32[]{:S(2)}) collective-permute-start(bf16[1152,512]{1,0:T(8,128)(2,1)} %add.536), channel_id=1, source_target_pairs={{8,16},{12,20},{16,8},{20,12},{9,17},{13,21},{17,9},{21,13},{10,18... | collective-permute-start | bytes 3538952 | tf_op jit(solution)/shard_map/ppermute | solution.py:74
  215.3 36.0 %collective-permute-start.20 = (bf16[576,1024]{1,0:T(8,128)(2,1)S(1)}, bf16[576,1024]{1,0:T(8,128)(2,1)}, u32[]{:S(2)}, u32[]{:S(2)}) collective-permute-start(bf16[576,1024]{1,0:T(8,128)(2,1)S(1)} %add_convert_fusion.4), channel_id=1, source_target_pairs={{0,8},{4,12},{24,16},{28,20},{1,9},{5,13},{25,17},{29,21},{2,10},{... | collective-permute-start | bytes 3538952 | tf_op jit(solution)/shard_map/ppermute | solution.py:74
  227.7 21.9 %collective-permute-start.23 = (bf16[256,1024]{1,0:T(8,128)(2,1)}, bf16[256,1024]{1,0:T(8,128)(2,1)}, u32[]{:S(2)}, u32[]{:S(2)}) collective-permute-start(bf16[256,1024]{1,0:T(8,128)(2,1)} %fusion.122), channel_id=1, source_target_pairs={{0,3},{1,2},{2,1},{3,0},{4,7},{5,6},{6,5},{7,4},{8,11},{9,10},{10,... | collective-permute-start | bytes 1572872 | tf_op jit(solution)/shard_map/ppermute | solution.py:25
  259.4 25.9 %collective-permute-start.32 = (bf16[256,1024]{1,0:T(8,128)(2,1)S(1)}, bf16[256,1024]{1,0:T(8,128)(2,1)S(1)}, u32[]{:S(2)}, u32[]{:S(2)}) collective-permute-start(bf16[256,1024]{1,0:T(8,128)(2,1)S(1)} %fusion.30), channel_id=1, source_target_pairs={{0,2},{1,3},{2,0},{3,1},{4,6},{5,7},{6,4},{7,5},{8,10},{9,11},{10,... | collective-permute-start | bytes 1572872 | tf_op jit(solution)/shard_map/ppermute | solution.py:25
  260.9 24.6 %collective-permute-start.33 = (bf16[256,1024]{1,0:T(8,128)(2,1)S(1)}, bf16[256,1024]{1,0:T(8,128)(2,1)S(1)}, u32[]{:S(2)}, u32[]{:S(2)}) collective-permute-start(bf16[256,1024]{1,0:T(8,128)(2,1)S(1)} %fusion.33), channel_id=1, source_target_pairs={{0,3},{1,2},{2,1},{3,0},{4,7},{5,6},{6,5},{7,4},{8,11},{9,10},{10,... | collective-permute-start | bytes 1572872 | tf_op jit(solution)/shard_map/ppermute | solution.py:25
  266.6 21.4 %collective-permute-start.26 = (bf16[576,1024]{1,0:T(8,128)(2,1)S(1)}, bf16[576,1024]{1,0:T(8,128)(2,1)S(1)}, u32[]{:S(2)}, u32[]{:S(2)}) collective-permute-start(bf16[576,1024]{1,0:T(8,128)(2,1)S(1)} %add.540), channel_id=1, source_target_pairs={{8,16},{12,20},{16,8},{20,12},{9,17},{13,21},{17,9},{21,13},{10,18... | collective-permute-start | bytes 3538952 | tf_op jit(solution)/shard_map/ppermute | solution.py:74
  273.1 30.0 %collective-permute-start.25 = (bf16[1152,512]{1,0:T(8,128)(2,1)S(1)}, bf16[1152,512]{1,0:T(8,128)(2,1)S(1)}, u32[]{:S(2)}, u32[]{:S(2)}) collective-permute-start(bf16[1152,512]{1,0:T(8,128)(2,1)S(1)} %add.539), channel_id=1, source_target_pairs={{16,24},{20,28},{8,0},{12,4},{17,25},{21,29},{9,1},{13,5},{18,26},... | collective-permute-start | bytes 3538952 | tf_op jit(solution)/shard_map/ppermute | solution.py:74
  274.4 30.0 %collective-permute-start.27 = (bf16[576,1024]{1,0:T(8,128)(2,1)S(1)}, bf16[576,1024]{1,0:T(8,128)(2,1)S(1)}, u32[]{:S(2)}, u32[]{:S(2)}) collective-permute-start(bf16[576,1024]{1,0:T(8,128)(2,1)S(1)} %add_convert_fusion.3), channel_id=1, source_target_pairs={{0,8},{4,12},{24,16},{28,20},{1,9},{5,13},{25,17},{29,21},{2,10},{... | collective-permute-start | bytes 3538952 | tf_op jit(solution)/shard_map/ppermute | solution.py:74
  305.8 38.8 %collective-permute-start.35 = (bf16[576,1024]{1,0:T(8,128)(2,1)}, bf16[576,1024]{1,0:T(8,128)(2,1)}, u32[]{:S(2)}, u32[]{:S(2)}) collective-permute-start(bf16[576,1024]{1,0:T(8,128)(2,1)} %add.556), channel_id=1, source_target_pairs={{8,16},{12,20},{16,8},{20,12},{9,17},{13,21},{17,9},{21,13},{10,18... | collective-permute-start | bytes 3538952 | tf_op jit(solution)/shard_map/ppermute | solution.py:74
  309.2 35.4 %collective-permute-start.34 = (bf16[576,1024]{1,0:T(8,128)(2,1)}, bf16[576,1024]{1,0:T(8,128)(2,1)}, u32[]{:S(2)}, u32[]{:S(2)}) collective-permute-start(bf16[576,1024]{1,0:T(8,128)(2,1)} %add.555), channel_id=1, source_target_pairs={{16,24},{20,28},{8,0},{12,4},{17,25},{21,29},{9,1},{13,5},{18,26},... | collective-permute-start | bytes 3538952 | tf_op jit(solution)/shard_map/ppermute | solution.py:74
  312.5 30.7 %collective-permute-start.36 = (bf16[512,1024]{1,0:T(8,128)(2,1)S(1)}, bf16[512,1024]{1,0:T(8,128)(2,1)}, u32[]{:S(2)}, u32[]{:S(2)}) collective-permute-start(bf16[512,1024]{1,0:T(8,128)(2,1)S(1)} %maximum_maximum_fusion), channel_id=1, source_target_pairs={{0,8},{4,12},{24,16},{28,20},{1,9},{5,13},{25,17},{29,21},{2,10},{... | collective-permute-start | bytes 3145736 | tf_op jit(solution)/shard_map/ppermute | solution.py:74
  348.2 21.8 %collective-permute-start.45 = (bf16[4,288,512]{2,1,0:T(8,128)(2,1)}, bf16[4,288,512]{2,1,0:T(8,128)(2,1)}, u32[]{:S(2)}, u32[]{:S(2)}) collective-permute-start(bf16[4,288,512]{2,1,0:T(8,128)(2,1)} %pad_maximum_fusion.8), channel_id=1, source_target_pairs={{0,4},{4,0},{8,12},{12,8},{16,20},{20,16},{24,28},{28,24},{1,5},{5... | collective-permute-start | bytes 3538952 | tf_op jit(solution)/shard_map/ppermute | solution.py:54
  350.5 28.6 %collective-permute-start.41 = (bf16[512,1024]{1,0:T(8,128)(2,1)S(1)}, bf16[512,1024]{1,0:T(8,128)(2,1)S(1)}, u32[]{:S(2)}, u32[]{:S(2)}) collective-permute-start(bf16[512,1024]{1,0:T(8,128)(2,1)S(1)} %add.565), channel_id=1, source_target_pairs={{8,16},{12,20},{16,8},{20,12},{9,17},{13,21},{17,9},{21,13},{10,18... | collective-permute-start | bytes 3145736 | tf_op jit(solution)/shard_map/ppermute | solution.py:74
  354.9 28.6 %collective-permute-start.40 = (bf16[576,1024]{1,0:T(8,128)(2,1)S(1)}, bf16[576,1024]{1,0:T(8,128)(2,1)S(1)}, u32[]{:S(2)}, u32[]{:S(2)}) collective-permute-start(bf16[576,1024]{1,0:T(8,128)(2,1)S(1)} %add.564), channel_id=1, source_target_pairs={{16,24},{20,28},{8,0},{12,4},{17,25},{21,29},{9,1},{13,5},{18,26},... | collective-permute-start | bytes 3538952 | tf_op jit(solution)/shard_map/ppermute | solution.py:74
  386.5 22.7 %all-to-all-start.2 = ((f32[4,5,256]{2,1,0:T(8,128)}), f32[4,5,256]{2,1,0:T(8,128)S(1)}, u32[]{:S(2)}, u32[]{:S(2)}) async-start(f32[4,5,256]{2,1,0:T(8,128)} %select_maximum_fusion.3), calls=%async_computation.2 | async-start | bytes 65536 | tf_op jit(solution)/shard_map/all_to_all | solution.py:95
  403.3 27.3 %collective-permute-start.49 = (bf16[512,1024]{1,0:T(8,128)(2,1)}, bf16[512,1024]{1,0:T(8,128)(2,1)}, u32[]{:S(2)}, u32[]{:S(2)}) collective-permute-start(bf16[512,1024]{1,0:T(8,128)(2,1)} %add.576), channel_id=1, source_target_pairs={{16,24},{20,28},{8,0},{12,4},{17,25},{21,29},{9,1},{13,5},{18,26},... | collective-permute-start | bytes 3145736 | tf_op jit(solution)/shard_map/ppermute | solution.py:74
  437.1 21.8 %collective-permute-start.58 = (bf16[4,576,256]{2,1,0:T(8,128)(2,1)}, bf16[4,576,256]{2,1,0:T(8,128)(2,1)}, u32[]{:S(2)}, u32[]{:S(2)}) collective-permute-start(bf16[4,576,256]{2,1,0:T(8,128)(2,1)} %pad_maximum_fusion.10), channel_id=1, source_target_pairs={{0,4},{4,0},{8,12},{12,8},{16,20},{20,16},{24,28},{28,24},{1,5},{5... | collective-permute-start | bytes 3538952 | tf_op jit(solution)/shard_map/ppermute | solution.py:54
  (142 other events, 1198.8 us)
Sparse Core Ops, SparseCore 0:
  24.4 28.5 all-gather.2
  55.2 70.5 all-gather.4

commit v2 on v1

--- a/solution.py
+++ b/solution.py
@@ -47,48 +47,6 @@
     devices = range(lax.axis_size("grp"))
     route = [(i - distance, i) for i in devices if i - distance in devices]
     return lax.ppermute(block, "grp", route)
-
-
-def exchange_core(block):
-    devices = range(lax.axis_size("grp"))
-    return lax.ppermute(block, "grp", [(i, i ^ 1) for i in devices])
-
-
-class Line:
-
-    def __init__(self, array):
-        self.chips = lax.axis_size("grp") // 2
-        self.array = array
-        self.total = 0.0
-        self.arrived = None
-        self.step = 1
-
-    def going(self):
-        return self.step < self.chips
-
-    def hop(self):
-        chips, step = self.chips, self.step
-        hops = [(step - 1, step), (chips - step, chips - 1 - step)]
-        route = [(2 * a + core, 2 * b + core) for a, b in hops for core in range(2)]
-        sent = self.array if step == 1 else self.array + self.arrived
-        return lax.ppermute(sent, "grp", route)
-
-    def take(self, arrived):
-        self.arrived = arrived
-        self.total = self.total + arrived.astype(full)
-        self.step += 1
-
-    def sum(self):
-        return (self.array.astype(full) + self.total).astype(half)
-
-
-def tick(lines, beside):
-    lines = [line for line in lines if line.going()]
-    hops = [line.hop() for line in lines]
-    hops, beside = lax.optimization_barrier((hops, beside))
-    for line, arrived in zip(lines, hops):
-        line.take(arrived)
-    return beside
 
 
 def swap_own(pieces):
@@ -259,44 +217,15 @@
     sig = jax.nn.sigmoid(gate)
     activated = gate * sig
     hidden = (activated * up).astype(half)
-    core = group % 2
-
-    def core_half(array, axis):
-        count = array.shape[axis] // 2
-        keep = lax.dynamic_slice_in_dim(array, core * count, count, axis)
-        send = lax.dynamic_slice_in_dim(array, (1 - core) * count, count, axis)
-        return (keep.astype(full) + exchange_core(send).astype(full)).astype(half)
-
-    def owner_blocks(array, axis):
-        count = array.shape[axis] // owners
-        return [
-            lax.dynamic_slice_in_dim(array, (owner ^ k) * count, count, axis)
-            for k in range(owners)
-        ]
-
-    def to_owner(blocks):
-        return [blocks[0]] + [exchange(blocks[k], k) for k in range(1, owners)]
-
-    def both_cores(blocks):
-        mine = jnp.stack([pick(place ^ owner, blocks) for place in range(owners)])
-        other = exchange_core(mine)
-        low = jnp.where(core == 0, mine, other)
-        high = jnp.where(core == 0, other, mine)
-        return low, high
-
-    def join_columns(halves, count):
-        both = jnp.concatenate(halves, 1).reshape(owners, -1, count, channels)
-        return both.transpose(1, 0, 2, 3).reshape(-1, channels)
-
-    def join_rows(halves, count):
-        both = jnp.concatenate(halves, 2).reshape(owners, share, count, width)
-        return both.transpose(1, 0, 2, 3).reshape(-1, width)
-
-    down_part = dot_tokens(hidden, cot_half).astype(half)
+
+    def scatter_grp(array, tiled):
+        return lax.psum_scatter(array, "grp", scatter_dimension=0, tiled=tiled)
+
+    down_part = dot_tokens(cot_half, hidden).astype(half)
     gate, up, down_part = lax.optimization_barrier((gate, up, down_part))
+    down_sum = scatter_grp(down_part, True)
     sig = jax.nn.sigmoid(gate)
     activated = gate * sig
-    down_line = Line(core_half(down_part, 1))
     grad_hidden = dot_rows(cot_half, down_half)
     grad_gate = (grad_hidden * up * sig * (1.0 + gate * (1.0 - sig))).astype(half)
     grad_up = (grad_hidden * activated).astype(half)
@@ -305,14 +234,15 @@
         return array[k * rows : (k + 1) * rows]
 
     gate_part = dot_tokens(grad_gate, normed_two).astype(half)
-    gate_line = Line(core_half(gate_part, 0))
     up_part = dot_tokens(grad_up, normed_two).astype(half)
-    up_line = Line(core_half(up_part, 0))
+    pair_part = jnp.concatenate(
+        [gate_part.reshape(groups, -1, width), up_part.reshape(groups, -1, width)], 1
+    )
+    pair_sum = scatter_grp(pair_part, False)
 
     grad_normed_two = scatter_own(
         lambda k: dot(block(grad_gate, k), gate_t) + dot(block(grad_up, k), up_t),
     )
-    grad_normed_two, gate_line.array = tick([down_line], (grad_normed_two, gate_line.array))
     gain_two_rows = jnp.sum(grad_normed_two * middle * inv_two, axis=0)
     weighted_two = gain_two_float * grad_normed_two
     grad_middle = (
@@ -325,9 +255,6 @@
         * jnp.mean(weighted_two * middle, axis=1, keepdims=True)
     )
     grad_middle_half = gather_own(grad_middle.astype(half))
-    grad_middle_half, up_line.array, hidden_late = tick(
-        [down_line, gate_line], (grad_middle_half, up_line.array, hidden)
-    )
     grad_mixed = dot_rows(grad_middle_half, out_half).reshape(owners, rows, channels)
     grad_c = grad_mixed * convolved
     grad_conv = grad_mixed * c_gate
@@ -356,30 +283,47 @@
         .astype(half)
         .reshape(owners * rows, 3 * channels)
     )
-    in_part = core_half(dot_tokens(grad_project, normed).astype(half), 0)
-    out_part = core_half(
-        dot_tokens(mixed.reshape(owners * rows, channels), grad_middle_half).astype(half), 1
-    )
-    in_rows, out_rows = in_part.shape[0], out_part.shape[0] // 2
-    out_part = jnp.concatenate([out_part[:out_rows], out_part[out_rows:]], 1)
-    last_line = Line(jnp.concatenate([in_part, out_part], 0))
+    in_part = dot_tokens(grad_project, normed).astype(half).reshape(groups, -1, width)
+    out_part = dot_tokens(grad_middle_half, mixed.reshape(owners * rows, channels)).astype(half)
+    out_part = out_part.reshape(groups, owners, -1, channels).transpose(0, 2, 1, 3)
+    last_part = jnp.concatenate([in_part, out_part.reshape(groups, -1, width)], 1)
+    last_sum = scatter_grp(last_part, False)
+
+    def columns_shard(pieces, parts):
+        cut = pieces.reshape(owners, parts, -1, channels)
+        return cut.transpose(1, 0, 2, 3).reshape(-1, channels)
+
+    def rows_shard(pieces):
+        cut = pieces.reshape(owners, -1, share, thin)
+        return cut.transpose(2, 0, 1, 3).reshape(-1, thin)
+
+    piece = run // groups
+    pair = pair_sum.reshape(-1, owners, channels).transpose(1, 0, 2)
+    down_rows = down_sum.T.reshape(owners, share, piece, thin).transpose(0, 2, 1, 3)
+    big = jnp.concatenate([pair, down_rows.reshape(owners, piece, channels)], 1)
+    big = swap_own(big)
+    big, hidden_late, project_late = lax.optimization_barrier((big, hidden, grad_project))
+    gate_shard = big[:, :piece].reshape(owners * piece, channels)
+    up_shard = big[:, piece : 2 * piece].reshape(owners * piece, channels)
+    down_shard = rows_shard(big[:, 2 * piece :])
+    big_all = jnp.concatenate(
+        [gate_shard, up_shard, big[:, 2 * piece :].reshape(-1, channels)], 0
+    )
+    big_all = lax.all_gather(big_all, "grp", axis=0, tiled=False)
+    split = 3 * sub
+    in_rows = last_sum[:split].reshape(split, owners, channels).transpose(1, 0, 2)
+    out_rows = last_sum[split:].reshape(-1, owners, channels).transpose(1, 0, 2)
+    out_rows = out_rows.reshape(thin, channels).T.reshape(owners, share, sub, thin)
+    out_rows = out_rows.transpose(0, 2, 1, 3).reshape(owners, sub, channels)
+    last = jnp.concatenate([in_rows, out_rows], 1)
+    last = swap_own(last)
+    in_shard = columns_shard(last[:, :split], 3)
+    out_shard = rows_shard(last[:, split:])
+    last_all = jnp.concatenate([in_shard, last[:, split:].reshape(-1, channels)], 0)
+    last_all = lax.all_gather(last_all, "grp", axis=0, tiled=False)
+    grad_normed = scatter_own(lambda k: dot(block(project_late, k), in_t))
     feed_out = scatter_own(lambda k: dot(block(hidden_late, k), down_half))
     block_out = (middle + feed_out).astype(half)
-    last_line.array, block_out, project_late = tick(
-        [down_line, gate_line, up_line], (last_line.array, block_out, grad_project)
-    )
-    grad_normed = scatter_own(lambda k: dot(block(project_late, k), in_t))
-
-    piece = run // groups
-    while down_line.going():
-        tick([down_line, gate_line, up_line, last_line], ())
-    down_blocks = to_owner(owner_blocks(down_line.sum(), 0))
-    down_blocks = tick([gate_line, up_line, last_line], down_blocks)
-    gate_blocks = to_owner(owner_blocks(gate_line.sum(), 1))
-    down_grad = join_rows(both_cores(down_blocks), piece)
-    gate_blocks, down_grad, grad_normed = tick(
-        [up_line, last_line], (gate_blocks, down_grad, grad_normed)
-    )
     inv_rms = lax.rsqrt(jnp.mean(x_float * x_float, axis=1, keepdims=True) + eps_norm)
     gain_rows = jnp.sum(grad_normed * x_float * inv_rms, axis=0)
     weighted = gain_float * grad_normed
@@ -401,70 +345,47 @@
     tap_share = tap_share.transpose(1, 2, 0, 3).reshape(taps, channels)
     gain_share = jnp.sum(pieces[:, taps:], axis=0)
     small_share = jnp.concatenate([tap_share, gain_share], 0)
-
-    up_blocks = to_owner(owner_blocks(up_line.sum(), 1))
-    gate_grad = join_columns(both_cores(gate_blocks), piece)
-    down_shard = lax.dynamic_slice_in_dim(down_grad, group * thin, thin, 1)
-    down_new = apply_adam(
-        w_down, moment_down, square_down, down_shard.astype(full), rate_matrix, decay_matrix
-    )
-    up_blocks, gate_grad, down_grad, down_new, grad_tokens, small_share = tick(
-        [last_line],
-        (up_blocks, gate_grad, down_grad.astype(full), down_new, grad_tokens, small_share),
-    )
-    up_grad = join_columns(both_cores(up_blocks), piece)
-    last = last_line.sum()
-    out_sum = jnp.concatenate([last[in_rows:, : width // 2], last[in_rows:, width // 2 :]], 0)
-    last_blocks = [
-        jnp.concatenate([wide] + jnp.split(rest, owners // 2, 1), 0)
-        for wide, rest in zip(owner_blocks(last[:in_rows], 1), owner_blocks(out_sum, 0))
-    ]
-    last_halves = both_cores(to_owner(last_blocks))
-    in_halves = [part[:, :in_rows] for part in last_halves]
-    out_halves = [
-        jnp.concatenate(jnp.split(part[:, in_rows:], owners // 2, 1), 2) for part in last_halves
-    ]
-    out_grad = join_rows(out_halves, sub)
-    in_grad = join_columns(in_halves, sub)
-    grad_w_down = down_grad
-    grad_w_out = out_grad.astype(full)
-
-    def turned(grad_t):
-        return lax.optimization_barrier(grad_t.T)
-
-    def my_rows(grad_t):
-        count = grad_t.shape[0] // groups
-        return turned(lax.dynamic_slice_in_dim(grad_t, group * count, count, 0))
-
-    grad_w_gate = turned(gate_grad).astype(full)
-    grad_w_up = turned(up_grad).astype(full)
-    grad_w_in = turned(in_grad).astype(full)
-
-    out_shard = lax.dynamic_slice_in_dim(out_grad, group * thin, thin, 1)
-    gate_shard = my_rows(gate_grad)
-    up_shard = my_rows(up_grad)
-    in_shard = my_rows(in_grad)
-
     for bit in range(groups.bit_length() - 1):
         route = [(i, i ^ (1 << bit)) for i in range(groups)]
         small_share = small_share + lax.ppermute(small_share, "grp", route)
+
+    def turned(grad_t):
+        return lax.optimization_barrier(grad_t.T)
+
+    def new_columns(shard_t, param, first, second):
+        shard = turned(shard_t).astype(full)
+        return apply_adam(param, first, second, shard, rate_matrix, decay_matrix)
+
+    def new_rows(shard, param, first, second):
+        return apply_adam(param, first, second, shard.astype(full), rate_matrix, decay_matrix)
+
+    gate_new = new_columns(gate_shard, w_gate, moment_gate, square_gate)
+    up_new = new_columns(up_shard, w_up, moment_up, square_up)
+    down_new = new_rows(down_shard, w_down, moment_down, square_down)
+
+    new_w_in, new_moment_in, new_square_in = new_columns(in_shard, w_in, moment_in, square_in)
+    new_w_out, new_moment_out, new_square_out = new_rows(
+        out_shard, w_out, moment_out, square_out
+    )
+    new_w_gate, new_moment_gate, new_square_gate = gate_new
+    new_w_up, new_moment_up, new_square_up = up_new
+    new_w_down, new_moment_down, new_square_down = down_new
+
+    def rows_whole(blocks):
+        cut = blocks.reshape(groups, -1, share, thin).transpose(2, 1, 0, 3)
+        return cut.reshape(-1, width).astype(full)
+
+    fan = 3 * width // groups
+    grad_w_in = turned(last_all[:, :fan].reshape(-1, channels)).astype(full)
+    grad_w_out = rows_whole(last_all[:, fan:])
+    count = owners * piece
+    grad_w_gate = turned(big_all[:, :count].reshape(-1, channels)).astype(full)
+    grad_w_up = turned(big_all[:, count : 2 * count].reshape(-1, channels)).astype(full)
+    grad_w_down = rows_whole(big_all[:, 2 * count :])
     grad_conv_w = small_share[:taps]
     grad_gain = small_share[taps]
     grad_gain_two = small_share[taps + 1]
 
-    new_w_in, new_moment_in, new_square_in = apply_adam(
-        w_in, moment_in, square_in, in_shard.astype(full), rate_matrix, decay_matrix
-    )
-    new_w_out, new_moment_out, new_square_out = apply_adam(
-        w_out, moment_out, square_out, out_shard.astype(full), rate_matrix, decay_matrix
-    )
-    new_w_gate, new_moment_gate, new_square_gate = apply_adam(
-        w_gate, moment_gate, square_gate, gate_shard.astype(full), rate_matrix, decay_matrix
-    )
-    new_w_up, new_moment_up, new_square_up = apply_adam(
-        w_up, moment_up, square_up, up_shard.astype(full), rate_matrix, decay_matrix
-    )
-    new_w_down, new_moment_down, new_square_down = down_new
     new_conv_w, new_moment_conv, new_square_conv = apply_adam(
         conv_w, moment_conv, square_conv, grad_conv_w, rate_vector, 0.0
     )

time: 491 us -> 541 us (1.10)
  waiting for transfers between devices: 156 us -> 244 us
  starting transfers between devices: 92.7 us -> 45.1 us
  other arithmetic: 80.9 us -> 49.5 us
  local copies, waits for them, and re-layouts: 47.7 us -> 77.1 us
  blocking collectives: 25.3 us -> 34.3 us
    reduce_scatter x0 -> x3, waiting for transfers between devices: none -> 106 us  [scatter_grp(): return lax.psum_scatter(array, 'grp', scatter_dimension=0, tiled=tiled)]
    ppermute x21 -> x0, waiting for transfers between devices: 46.3 us -> none  [the longest x12 45.9 us: hop(): return lax.ppermute(sent, 'grp', route)]
    ppermute x21 -> x0, starting transfers between devices: 43.7 us -> none  [the longest x12 36.3 us: hop(): return lax.ppermute(sent, 'grp', route)]
    ppermute x36 -> x24, waiting for transfers between devices: 99 us -> 116 us  [exchange(): return lax.ppermute(block, 'own', [(i, i ^ k) for i in devices])]
    convert_element_type x0 -> x8, local copies, waits for them, and re-layouts: none -> 15.8 us  [the longest x4 15.4 us: rows_whole(): return cut.reshape(-1, width).astype(full)]
    another operation x17 -> x5, other arithmetic: 17.9 us -> 2.58 us  [the longest x12 15.3 us: both_cores(): mine = jnp.stack([pick(place ^ owner, blocks) for place in range(owners)])]
    ppermute x36 -> x24, starting transfers between devices: 42.5 us -> 29.1 us  [exchange(): return lax.ppermute(block, 'own', [(i, i ^ k) for i in devices])]
    add x8 -> x0, other arithmetic: 12.9 us -> none  [hop(): sent = self.array if step == 1 else self.array + self.arrived]
  transfers between devices with their start and end apart: 65 -> 38, of which waited for: 28 -> 21; matrix products, arithmetic and copies ran while one was open for 26% -> 21% of each run, Pallas kernels for 0% -> 0%
where the time goes in v2:
time: 541 us; the launch traced here: 534 us
  waiting for transfers between devices  244 us (45%)
  local copies, waits for them, and re-layouts  77.1 us (14%)
  matrix products  68 us (13%)
  other arithmetic  49.5 us (9%)
  starting transfers between devices  45.1 us (8%)
  blocking collectives  34.3 us (6%)
  between operations  16.2 us (3%)
    ppermute x24, waiting for transfers between devices, exchange(): return lax.ppermute(block, 'own', [(i, i ^ k) for i in devices])  116 us
    reduce_scatter x3, waiting for transfers between devices, scatter_grp(): return lax.psum_scatter(array, 'grp', scatter_dimension=0, tiled=tiled)  106 us
    unnamed x177, local copies, waits for them, and re-layouts  36.5 us
    all_to_all x3, blocking collectives, swap_own(): return lax.all_to_all(pieces, 'own', 0, 0, tiled=True)  34.3 us
    dot_general x20, matrix products, dot(): return jnp.dot(left, right, preferred_element_type=full)  29.6 us
    ppermute x24, starting transfers between devices, exchange(): return lax.ppermute(block, 'own', [(i, i ^ k) for i in devices])  29.1 us
    dot_general x5, matrix products, dot_rows(): lax.dot_general(left, right, (((1,), (1,)), ((), ())), preferred_element_...  20.8 us
    dot_general x5, matrix products, dot_tokens(): lax.dot_general(left, right, (((0,), (0,)), ((), ())), preferred_element_...  17.6 us
  transfers between devices with their start and end apart: 38, of which 21 were waited for; matrix products, arithmetic and copies ran while one was open for 21% of the time, Pallas kernels for 0%

profile of v2, /device:TPU:0, one launch (start us, length us, event | category | flops | bytes accessed | tf_op | source)
XLA Modules:
  0.0 533.7 jit_solution(15653894484757714643)
XLA Ops:
  11.7 11.3 %all_to_all.25 = bf16[4,133,256]{2,1,0:T(8,128)(2,1)S(1)} all-to-all(bf16[4,133,256]{2,1,0:T(8,128)(2,1)S(1)} %pad_maximum_fusion.13), channel_id=1, replica_groups=mesh['grp'=8,'own'=4] {'own'}, dimensions={0} | all-to-all | bytes 544768 | tf_op jit(solution)/shard_map/all_to_all | solution.py:53
  24.9 14.0 %all_to_all.26 = bf16[4,432,256]{2,1,0:T(8,128)(2,1)S(1)} all-to-all(bf16[4,432,256]{2,1,0:T(8,128)(2,1)S(1)} %pad_maximum_fusion.10), channel_id=1, replica_groups=mesh['grp'=8,'own'=4] {'own'}, dimensions={0} | all-to-all | bytes 1769472 | tf_op jit(solution)/shard_map/all_to_all | solution.py:53
  45.5 11.8 %collective-permute-done.2 = bf16[256,1024]{1,0:T(8,128)(2,1)S(1)} collective-permute-done((bf16[256,1024]{1,0:T(8,128)(2,1)S(1)}, bf16[256,1024]{1,0:T(8,128)(2,1)S(1)}, u32[]{:S(2)}, u32[]{:S(2)}) %collective-permute-start.2) | collective-permute-done | bytes 524320 | tf_op jit(solution)/shard_map/ppermute | solution.py:25
  57.3 7.7 %collective-permute-done.1 = bf16[256,1024]{1,0:T(8,128)(2,1)S(1)} collective-permute-done((bf16[256,1024]{1,0:T(8,128)(2,1)S(1)}, bf16[256,1024]{1,0:T(8,128)(2,1)S(1)}, u32[]{:S(2)}, u32[]{:S(2)}) %collective-permute-start.1) | collective-permute-done | bytes 524320 | tf_op jit(solution)/shard_map/ppermute | solution.py:25
  90.7 3.8 collective-permute-done.6
  94.5 13.3 %collective-permute-done.5 = bf16[256,1024]{1,0:T(8,128)(2,1)S(1)} collective-permute-done((bf16[256,1024]{1,0:T(8,128)(2,1)S(1)}, bf16[256,1024]{1,0:T(8,128)(2,1)S(1)}, u32[]{:S(2)}, u32[]{:S(2)}) %collective-permute-start.5) | collective-permute-done | bytes 524320 | tf_op jit(solution)/shard_map/ppermute | solution.py:25
  112.9 4.1 collective-permute-done.9
  117.9 7.8 %all-gather.9.cloned.1.call-done = bf16[8,432,1024]{2,1,0:T(8,128)(2,1)} async-done(((bf16[1,432,1024]{2,1,0:T(8,128)(2,1)}), bf16[8,432,1024]{2,1,0:T(8,128)(2,1)}) %all-gather.9.cloned.1.call-update) | async-done | bytes 7077904 | tf_op jit(solution)/shard_map/all_gather | solution.py:172
  125.7 4.1 fusion.123
  133.5 7.3 %collective-permute-done.11 = bf16[256,1024]{1,0:T(8,128)(2,1)} collective-permute-done((bf16[256,1024]{1,0:T(8,128)(2,1)}, bf16[256,1024]{1,0:T(8,128)(2,1)}, u32[]{:S(2)}, u32[]{:S(2)}) %collective-permute-start.11) | collective-permute-done | bytes 524320 | tf_op jit(solution)/shard_map/ppermute | solution.py:25
  140.7 4.4 fusion.108
  145.2 8.3 %multiply_convert_fusion.2 = (bf16[1024,1152]{1,0:T(8,128)(2,1)S(1)}, f32[1024,1152]{1,0:T(8,128)}) fusion(f32[1024,1152]{1,0:T(8,128)S(1)} %fusion.108, bf16[1152,1024]{1,0:T(8,128)(2,1)S(1)} %bitcast.267, bf16[256,1024]{1,0:T(8,128)(2,1)} %collective-permute-done.12, bf16[256,1024]{1,0:T(8,128)(2,1)} %collective-permute-done.11, ...), kind=kOutput, calls=%fused_computation.7 | convolution fusion | flops 2431385600 | bytes 16252928 | tf_op jit(solution)/shard_map/dot_general | solution.py:82
  155.0 6.4 %convolution_convert_fusion.2 = bf16[1024,1152]{1,0:T(8,128)(2,1)} fusion(bf16[1024,1024]{1,0:T(8,128)(2,1)} %constant_dynamic-update-slice_fusion, bf16[1024,1152]{1,0:T(8,128)(2,1)S(1)} %get-tuple-element.51), kind=kOutput, calls=%fused_computation.13 | convolution fusion | flops 2417098752 | bytes 6815744 | tf_op jit(solution)/shard_map/dot_general | solution.py:86
  161.4 5.4 %fusion.11 = f32[1024,1152]{1,0:T(8,128)S(1)} fusion(bf16[1024,1024]{1,0:T(8,128)(2,1)} %constant_dynamic-update-slice_fusion, bf16[144,8,8,128]{3,2,1,0:T(8,128)(2,1)} %bitcast.304), kind=kOutput, calls=%fused_computation.22 | convolution fusion | flops 2415919104 | bytes 9175040 | tf_op jit(solution)/shard_map/dot_general | solution.py:82
  178.9 9.5 %collective-permute-done.15 = bf16[256,1024]{1,0:T(8,128)(2,1)S(1)} collective-permute-done((bf16[256,1024]{1,0:T(8,128)(2,1)S(1)}, bf16[256,1024]{1,0:T(8,128)(2,1)S(1)}, u32[]{:S(2)}, u32[]{:S(2)}) %collective-permute-start.15) | collective-permute-done | bytes 524320 | tf_op jit(solution)/shard_map/ppermute | solution.py:25
  188.4 10.3 %collective-permute-done.14 = bf16[256,1024]{1,0:T(8,128)(2,1)S(1)} collective-permute-done((bf16[256,1024]{1,0:T(8,128)(2,1)S(1)}, bf16[256,1024]{1,0:T(8,128)(2,1)S(1)}, u32[]{:S(2)}, u32[]{:S(2)}) %collective-permute-start.14) | collective-permute-done | bytes 524320 | tf_op jit(solution)/shard_map/ppermute | solution.py:25
  206.3 12.0 %collective-permute-done.18 = bf16[256,1024]{1,0:T(8,128)(2,1)S(1)} collective-permute-done((bf16[256,1024]{1,0:T(8,128)(2,1)S(1)}, bf16[256,1024]{1,0:T(8,128)(2,1)S(1)}, u32[]{:S(2)}, u32[]{:S(2)}) %collective-permute-start.18) | collective-permute-done | bytes 524320 | tf_op jit(solution)/shard_map/ppermute | solution.py:25
  218.3 10.3 %collective-permute-done.17 = bf16[256,1024]{1,0:T(8,128)(2,1)} collective-permute-done((bf16[256,1024]{1,0:T(8,128)(2,1)S(1)}, bf16[256,1024]{1,0:T(8,128)(2,1)}, u32[]{:S(2)}, u32[]{:S(2)}) %collective-permute-start.17) | collective-permute-done | bytes 524320 | tf_op jit(solution)/shard_map/ppermute | solution.py:25
  242.9 4.3 convolution_convert_fusion
  247.2 4.2 convolution_convert_fusion.1
  254.1 25.8 %reduce-scatter.8.cloned.1.call-done = bf16[1,128,1024]{2,1,0:T(8,128)(2,1)} async-done(((bf16[8,128,1024]{2,1,0:T(8,128)(2,1)}), bf16[1,128,1024]{2,1,0:T(8,128)(2,1)}) %reduce-scatter.8.cloned.1.call-update) | async-done | bytes 262160 | tf_op jit(solution)/shard_map/reduce_scatter | solution.py:222
  282.4 9.0 %all_to_all.27 = bf16[4,128,256]{2,1,0:T(8,128)(2,1)S(1)} all-to-all(bf16[4,128,256]{2,1,0:T(8,128)(2,1)S(1)} %copy.233), channel_id=1, replica_groups=mesh['grp'=8,'own'=4] {'own'}, dimensions={0} | all-to-all | bytes 524288 | tf_op jit(solution)/shard_map/all_to_all | solution.py:53
  292.9 25.1 %reduce-scatter.6.cloned.1.call-done = bf16[128,1152]{1,0:T(8,128)(2,1)} async-done(((bf16[1024,1152]{1,0:T(8,128)(2,1)}), bf16[128,1152]{1,0:T(8,128)(2,1)}) %reduce-scatter.6.cloned.1.call-update) | async-done | bytes 294928 | tf_op jit(solution)/shard_map/reduce_scatter | solution.py:222
  319.6 54.9 %reduce-scatter.4.cloned.1.call-done = bf16[1,288,1024]{2,1,0:T(8,128)(2,1)} async-done(((bf16[8,288,1024]{2,1,0:T(8,128)(2,1)}), bf16[1,288,1024]{2,1,0:T(8,128)(2,1)}) %reduce-scatter.4.cloned.1.call-update) | async-done | bytes 589840 | tf_op jit(solution)/shard_map/reduce_scatter | solution.py:222
  383.0 8.6 %all-to-all-done.2 = bf16[4,432,256]{2,1,0:T(8,128)(2,1)S(1)} async-done(((bf16[4,432,256]{2,1,0:T(8,128)(2,1)}), bf16[4,432,256]{2,1,0:T(8,128)(2,1)S(1)}, u32[]{:S(2)}, u32[]{:S(2)}) %all-to-all-start.2) | async-done | bytes 884768 | tf_op jit(solution)/shard_map/all_to_all | solution.py:53
  441.4 6.3 %collective-permute-done.25 = bf16[256,1024]{1,0:T(8,128)(2,1)} collective-permute-done((bf16[256,1024]{1,0:T(8,128)(2,1)}, bf16[256,1024]{1,0:T(8,128)(2,1)}, u32[]{:S(2)}, u32[]{:S(2)}) %collective-permute-start.25) | collective-permute-done | bytes 524320 | tf_op jit(solution)/shard_map/ppermute | solution.py:25
  449.2 19.4 %collective-permute-done.24 = bf16[256,1024]{1,0:T(8,128)(2,1)} collective-permute-done((bf16[256,1024]{1,0:T(8,128)(2,1)}, bf16[256,1024]{1,0:T(8,128)(2,1)}, u32[]{:S(2)}, u32[]{:S(2)}) %collective-permute-start.24) | collective-permute-done | bytes 524320 | tf_op jit(solution)/shard_map/ppermute | solution.py:25
  481.4 4.1 add_convert_fusion
  497.0 6.8 %slice_convert_fusion = (f32[8,576,256]{2,1,0:T(8,128)}, bf16[8,576,256]{2,1,0:T(8,128)(2,1)S(1)}, bf16[8,576,256]{2,1,0:T(8,128)(2,1)}) fusion(bf16[8,1728,256]{2,1,0:T(8,128)(2,1)} %bitcast.293), kind=kLoop, calls=%fused_computation.24 | loop fusion | flops 1179648 | bytes 16515072 | tf_op jit(solution)/shard_map/convert_element_type | solution.py:376
  503.8 4.5 copy.246
  511.3 6.8 %reshape.499 = f32[8,576,2,128]{3,2,1,0:T(2,128)} reshape(f32[8,576,256]{2,1,0:T(8,128)} %get-tuple-element.270) | data formatting | bytes 9437184 | tf_op jit(solution)/shard_map/convert_element_type | solution.py:376
  518.0 5.1 copy.237
  (412 shorter events, 180.6 us)
Async XLA Ops:
  7.2 62.3 %all-gather.7.cloned.1.call-start = ((), (), s32[]{:S(2)}) async-start(), calls=%async_computation.8 | async-start | bytes 2359296 | tf_op jit(solution)/shard_map/all_gather | solution.py:162
  24.1 101.6 %all-gather.9.cloned.1.call-start = ((), (), s32[]{:S(2)}) async-start(), calls=%async_computation.9 | async-start | bytes 7962624 | tf_op jit(solution)/shard_map/all_gather | solution.py:172
  40.9 239.0 %reduce-scatter.8.cloned.1.call-start = ((), (), s32[]{:S(2)}) async-start(), calls=%async_computation.12 | async-start | bytes 2359296 | tf_op jit(solution)/shard_map/reduce_scatter | solution.py:222
  41.6 15.8 %collective-permute-start.2 = (bf16[256,1024]{1,0:T(8,128)(2,1)S(1)}, bf16[256,1024]{1,0:T(8,128)(2,1)S(1)}, u32[]{:S(2)}, u32[]{:S(2)}) collective-permute-start(bf16[256,1024]{1,0:T(8,128)(2,1)S(1)} %copy-done.22), channel_id=1, source_target_pairs={{0,3},{1,2},{2,1},{3,0},{4,7},{5,6},{6,5},{7,4},{8,11},{9,10},{10,... | collective-permute-start | bytes 1572872 | tf_op jit(solution)/shard_map/ppermute | solution.py:25
  42.4 22.6 %collective-permute-start.1 = (bf16[256,1024]{1,0:T(8,128)(2,1)S(1)}, bf16[256,1024]{1,0:T(8,128)(2,1)S(1)}, u32[]{:S(2)}, u32[]{:S(2)}) collective-permute-start(bf16[256,1024]{1,0:T(8,128)(2,1)S(1)} %copy-done.22), channel_id=1, source_target_pairs={{0,2},{1,3},{2,0},{3,1},{4,6},{5,7},{6,4},{7,5},{8,10},{9,11},{10,... | collective-permute-start | bytes 1572872 | tf_op jit(solution)/shard_map/ppermute | solution.py:25
  43.9 21.9 %collective-permute-start = (bf16[256,1024]{1,0:T(8,128)(2,1)S(1)}, bf16[256,1024]{1,0:T(8,128)(2,1)}, u32[]{:S(2)}, u32[]{:S(2)}) collective-permute-start(bf16[256,1024]{1,0:T(8,128)(2,1)S(1)} %copy-done.22), channel_id=1, source_target_pairs={{0,1},{1,0},{2,3},{3,2},{4,5},{5,4},{6,7},{7,6},{8,9},{9,8},{10,11... | collective-permute-start | bytes 1572872 | tf_op jit(solution)/shard_map/ppermute | solution.py:25
  67.2 18.1 %collective-permute-start.7 = (bf16[256,1024]{1,0:T(8,128)(2,1)}, bf16[256,1024]{1,0:T(8,128)(2,1)}, u32[]{:S(2)}, u32[]{:S(2)}) collective-permute-start(bf16[256,1024]{1,0:T(8,128)(2,1)} %param.28), channel_id=1, source_target_pairs={{0,1},{1,0},{2,3},{3,2},{4,5},{5,4},{6,7},{7,6},{8,9},{9,8},{10,11... | collective-permute-start | bytes 1572872 | tf_op jit(solution)/shard_map/ppermute | solution.py:25
  68.6 20.3 %collective-permute-start.8 = (bf16[256,1024]{1,0:T(8,128)(2,1)}, bf16[256,1024]{1,0:T(8,128)(2,1)}, u32[]{:S(2)}, u32[]{:S(2)}) collective-permute-start(bf16[256,1024]{1,0:T(8,128)(2,1)} %param.28), channel_id=1, source_target_pairs={{0,2},{1,3},{2,0},{3,1},{4,6},{5,7},{6,4},{7,5},{8,10},{9,11},{10,... | collective-permute-start | bytes 1572872 | tf_op jit(solution)/shard_map/ppermute | solution.py:25
  79.9 14.7 %collective-permute-start.6 = (bf16[256,1024]{1,0:T(8,128)(2,1)S(1)}, bf16[256,1024]{1,0:T(8,128)(2,1)S(1)}, u32[]{:S(2)}, u32[]{:S(2)}) collective-permute-start(bf16[256,1024]{1,0:T(8,128)(2,1)S(1)} %convolution_convert_fusion.4), channel_id=1, source_target_pairs={{0,3},{1,2},{2,1},{3,0},{4,7},{5,6},{6,5},{7,4},{8,11},{9,10},{10,... | collective-permute-start | bytes 1572872 | tf_op jit(solution)/shard_map/ppermute | solution.py:25
  81.6 26.3 %collective-permute-start.5 = (bf16[256,1024]{1,0:T(8,128)(2,1)S(1)}, bf16[256,1024]{1,0:T(8,128)(2,1)S(1)}, u32[]{:S(2)}, u32[]{:S(2)}) collective-permute-start(bf16[256,1024]{1,0:T(8,128)(2,1)S(1)} %convolution_convert_fusion.5), channel_id=1, source_target_pairs={{0,2},{1,3},{2,0},{3,1},{4,6},{5,7},{6,4},{7,5},{8,10},{9,11},{10,... | collective-permute-start | bytes 1572872 | tf_op jit(solution)/shard_map/ppermute | solution.py:25
  82.9 25.0 %collective-permute-start.4 = (bf16[256,1024]{1,0:T(8,128)(2,1)S(1)}, bf16[256,1024]{1,0:T(8,128)(2,1)S(1)}, u32[]{:S(2)}, u32[]{:S(2)}) collective-permute-start(bf16[256,1024]{1,0:T(8,128)(2,1)S(1)} %convolution_convert_fusion.6), channel_id=1, source_target_pairs={{0,1},{1,0},{2,3},{3,2},{4,5},{5,4},{6,7},{7,6},{8,9},{9,8},{10,11... | collective-permute-start | bytes 1572872 | tf_op jit(solution)/shard_map/ppermute | solution.py:25
  85.3 31.7 %collective-permute-start.9 = (bf16[256,1024]{1,0:T(8,128)(2,1)}, bf16[256,1024]{1,0:T(8,128)(2,1)S(1)}, u32[]{:S(2)}, u32[]{:S(2)}) collective-permute-start(bf16[256,1024]{1,0:T(8,128)(2,1)} %param.28), channel_id=1, source_target_pairs={{0,3},{1,2},{2,1},{3,0},{4,7},{5,6},{6,5},{7,4},{8,11},{9,10},{10,... | collective-permute-start | bytes 1572872 | tf_op jit(solution)/shard_map/ppermute | solution.py:25
  109.4 24.0 %collective-permute-start.12 = (bf16[256,1024]{1,0:T(8,128)(2,1)}, bf16[256,1024]{1,0:T(8,128)(2,1)}, u32[]{:S(2)}, u32[]{:S(2)}) collective-permute-start(bf16[256,1024]{1,0:T(8,128)(2,1)} %multiply_convert_fusion.6), channel_id=1, source_target_pairs={{0,3},{1,2},{2,1},{3,0},{4,7},{5,6},{6,5},{7,4},{8,11},{9,10},{10,... | collective-permute-start | bytes 1572872 | tf_op jit(solution)/shard_map/ppermute | solution.py:25
  111.2 29.5 %collective-permute-start.11 = (bf16[256,1024]{1,0:T(8,128)(2,1)}, bf16[256,1024]{1,0:T(8,128)(2,1)}, u32[]{:S(2)}, u32[]{:S(2)}) collective-permute-start(bf16[256,1024]{1,0:T(8,128)(2,1)} %multiply_convert_fusion.6), channel_id=1, source_target_pairs={{0,2},{1,3},{2,0},{3,1},{4,6},{5,7},{6,4},{7,5},{8,10},{9,11},{10,... | collective-permute-start | bytes 1572872 | tf_op jit(solution)/shard_map/ppermute | solution.py:25
  112.5 28.2 %collective-permute-start.10 = (bf16[256,1024]{1,0:T(8,128)(2,1)}, bf16[256,1024]{1,0:T(8,128)(2,1)}, u32[]{:S(2)}, u32[]{:S(2)}) collective-permute-start(bf16[256,1024]{1,0:T(8,128)(2,1)} %multiply_convert_fusion.6), channel_id=1, source_target_pairs={{0,1},{1,0},{2,3},{3,2},{4,5},{5,4},{6,7},{7,6},{8,9},{9,8},{10,11... | collective-permute-start | bytes 1572872 | tf_op jit(solution)/shard_map/ppermute | solution.py:25
  172.6 15.8 %collective-permute-start.15 = (bf16[256,1024]{1,0:T(8,128)(2,1)S(1)}, bf16[256,1024]{1,0:T(8,128)(2,1)S(1)}, u32[]{:S(2)}, u32[]{:S(2)}) collective-permute-start(bf16[256,1024]{1,0:T(8,128)(2,1)S(1)} %fusion.24), channel_id=1, source_target_pairs={{0,3},{1,2},{2,1},{3,0},{4,7},{5,6},{6,5},{7,4},{8,11},{9,10},{10,... | collective-permute-start | bytes 1572872 | tf_op jit(solution)/shard_map/ppermute | solution.py:25
  175.2 23.6 %collective-permute-start.14 = (bf16[256,1024]{1,0:T(8,128)(2,1)S(1)}, bf16[256,1024]{1,0:T(8,128)(2,1)S(1)}, u32[]{:S(2)}, u32[]{:S(2)}) collective-permute-start(bf16[256,1024]{1,0:T(8,128)(2,1)S(1)} %fusion.23), channel_id=1, source_target_pairs={{0,2},{1,3},{2,0},{3,1},{4,6},{5,7},{6,4},{7,5},{8,10},{9,11},{10,... | collective-permute-start | bytes 1572872 | tf_op jit(solution)/shard_map/ppermute | solution.py:25
  177.4 21.3 %collective-permute-start.13 = (bf16[256,1024]{1,0:T(8,128)(2,1)S(1)}, bf16[256,1024]{1,0:T(8,128)(2,1)S(1)}, u32[]{:S(2)}, u32[]{:S(2)}) collective-permute-start(bf16[256,1024]{1,0:T(8,128)(2,1)S(1)} %fusion.22), channel_id=1, source_target_pairs={{0,1},{1,0},{2,3},{3,2},{4,5},{5,4},{6,7},{7,6},{8,9},{9,8},{10,11... | collective-permute-start | bytes 1572872 | tf_op jit(solution)/shard_map/ppermute | solution.py:25
  202.5 15.8 %collective-permute-start.18 = (bf16[256,1024]{1,0:T(8,128)(2,1)S(1)}, bf16[256,1024]{1,0:T(8,128)(2,1)S(1)}, u32[]{:S(2)}, u32[]{:S(2)}) collective-permute-start(bf16[256,1024]{1,0:T(8,128)(2,1)S(1)} %fusion.106), channel_id=1, source_target_pairs={{0,3},{1,2},{2,1},{3,0},{4,7},{5,6},{6,5},{7,4},{8,11},{9,10},{10,... | collective-permute-start | bytes 1572872 | tf_op jit(solution)/shard_map/ppermute | solution.py:25
  204.2 24.5 %collective-permute-start.17 = (bf16[256,1024]{1,0:T(8,128)(2,1)S(1)}, bf16[256,1024]{1,0:T(8,128)(2,1)}, u32[]{:S(2)}, u32[]{:S(2)}) collective-permute-start(bf16[256,1024]{1,0:T(8,128)(2,1)S(1)} %fusion.106), channel_id=1, source_target_pairs={{0,2},{1,3},{2,0},{3,1},{4,6},{5,7},{6,4},{7,5},{8,10},{9,11},{10,... | collective-permute-start | bytes 1572872 | tf_op jit(solution)/shard_map/ppermute | solution.py:25
  205.4 23.2 %collective-permute-start.16 = (bf16[256,1024]{1,0:T(8,128)(2,1)S(1)}, bf16[256,1024]{1,0:T(8,128)(2,1)}, u32[]{:S(2)}, u32[]{:S(2)}) collective-permute-start(bf16[256,1024]{1,0:T(8,128)(2,1)S(1)} %fusion.106), channel_id=1, source_target_pairs={{0,1},{1,0},{2,3},{3,2},{4,5},{5,4},{6,7},{7,6},{8,9},{9,8},{10,11... | collective-permute-start | bytes 1572872 | tf_op jit(solution)/shard_map/ppermute | solution.py:25
  241.2 76.7 %reduce-scatter.6.cloned.1.call-start = ((), (), s32[]{:S(2)}) async-start(), calls=%async_computation.11 | async-start | bytes 2654208 | tf_op jit(solution)/shard_map/reduce_scatter | solution.py:222
  241.8 132.7 %reduce-scatter.4.cloned.1.call-start = ((), (), s32[]{:S(2)}) async-start(), calls=%async_computation.10 | async-start | bytes 5308416 | tf_op jit(solution)/shard_map/reduce_scatter | solution.py:222
  254.1 151.1 %all-gather.11.cloned.1.call-start = ((), (), s32[]{:S(2)}) async-start(), calls=%async_computation.13 | async-start | bytes 2359296 | tf_op jit(solution)/shard_map/all_gather | solution.py:323
  377.9 13.8 %all-to-all-start.2 = ((bf16[4,432,256]{2,1,0:T(8,128)(2,1)}), bf16[4,432,256]{2,1,0:T(8,128)(2,1)S(1)}, u32[]{:S(2)}, u32[]{:S(2)}) async-start(bf16[4,432,256]{2,1,0:T(8,128)(2,1)} %copy.227), calls=%async_computation.4 | async-start | bytes 1769472 | tf_op jit(solution)/shard_map/all_to_all | solution.py:53
  381.5 115.4 %all-gather.13.cloned.1.call-start = ((), (), s32[]{:S(2)}) async-start(), calls=%async_computation.14 | async-start | bytes 7962624 | tf_op jit(solution)/shard_map/all_gather | solution.py:312
  420.4 60.9 %collective-permute-start.22 = (bf16[256,1024]{1,0:T(8,128)(2,1)}, bf16[256,1024]{1,0:T(8,128)(2,1)}, u32[]{:S(2)}, u32[]{:S(2)}) collective-permute-start(bf16[256,1024]{1,0:T(8,128)(2,1)} %fusion.19), channel_id=1, source_target_pairs={{0,3},{1,2},{2,1},{3,0},{4,7},{5,6},{6,5},{7,4},{8,11},{9,10},{10,... | collective-permute-start | bytes 1572872 | tf_op jit(solution)/shard_map/ppermute | solution.py:25
  424.5 56.8 %collective-permute-start.21 = (bf16[256,1024]{1,0:T(8,128)(2,1)}, bf16[256,1024]{1,0:T(8,128)(2,1)}, u32[]{:S(2)}, u32[]{:S(2)}) collective-permute-start(bf16[256,1024]{1,0:T(8,128)(2,1)} %fusion.16), channel_id=1, source_target_pairs={{0,2},{1,3},{2,0},{3,1},{4,6},{5,7},{6,4},{7,5},{8,10},{9,11},{10,... | collective-permute-start | bytes 1572872 | tf_op jit(solution)/shard_map/ppermute | solution.py:25
  427.4 20.3 %collective-permute-start.25 = (bf16[256,1024]{1,0:T(8,128)(2,1)}, bf16[256,1024]{1,0:T(8,128)(2,1)}, u32[]{:S(2)}, u32[]{:S(2)}) collective-permute-start(bf16[256,1024]{1,0:T(8,128)(2,1)} %convolution_convert_fusion.8), channel_id=1, source_target_pairs={{0,3},{1,2},{2,1},{3,0},{4,7},{5,6},{6,5},{7,4},{8,11},{9,10},{10,... | collective-permute-start | bytes 1572872 | tf_op jit(solution)/shard_map/ppermute | solution.py:25
  430.3 38.3 %collective-permute-start.24 = (bf16[256,1024]{1,0:T(8,128)(2,1)}, bf16[256,1024]{1,0:T(8,128)(2,1)}, u32[]{:S(2)}, u32[]{:S(2)}) collective-permute-start(bf16[256,1024]{1,0:T(8,128)(2,1)} %convolution_convert_fusion.9), channel_id=1, source_target_pairs={{0,2},{1,3},{2,0},{3,1},{4,6},{5,7},{6,4},{7,5},{8,10},{9,11},{10,... | collective-permute-start | bytes 1572872 | tf_op jit(solution)/shard_map/ppermute | solution.py:25
  432.2 36.4 %collective-permute-start.23 = (bf16[256,1024]{1,0:T(8,128)(2,1)}, bf16[256,1024]{1,0:T(8,128)(2,1)}, u32[]{:S(2)}, u32[]{:S(2)}) collective-permute-start(bf16[256,1024]{1,0:T(8,128)(2,1)} %convolution_convert_fusion.10), channel_id=1, source_target_pairs={{0,1},{1,0},{2,3},{3,2},{4,5},{5,4},{6,7},{7,6},{8,9},{9,8},{10,11... | collective-permute-start | bytes 1572872 | tf_op jit(solution)/shard_map/ppermute | solution.py:25
  447.7 33.6 %collective-permute-start.20 = (bf16[256,1024]{1,0:T(8,128)(2,1)}, bf16[256,1024]{1,0:T(8,128)(2,1)}, u32[]{:S(2)}, u32[]{:S(2)}) collective-permute-start(bf16[256,1024]{1,0:T(8,128)(2,1)} %fusion.13), channel_id=1, source_target_pairs={{0,1},{1,0},{2,3},{3,2},{4,5},{5,4},{6,7},{7,6},{8,9},{9,8},{10,11... | collective-permute-start | bytes 1572872 | tf_op jit(solution)/shard_map/ppermute | solution.py:25
  (87 other events, 630.6 us)
Sparse Core Ops, SparseCore 0:
  24.3 28.5 all-gather.6
  55.1 70.5 all-gather.8
  241.4 38.5 reduce-scatter.7
  282.1 35.7 reduce-scatter.5
  320.7 53.7 reduce-scatter.3
  376.5 27.6 all-gather.10
  405.8 70.5 all-gather.12
